TPU v7x, 512 devices: a whole 4x8x8 slice. The times are simulated.
512 devices in a mesh: band: 16 (over x, y_hi), grid: 32 (over y_lo, z, core).
Axes of the slice: x: 4, y: 8 (y_hi: 4, y_lo: 2; y = y_hi * 2 + y_lo), z: 8, core: 2. Of those that a mesh axis runs over, the one named last changes fastest.
Arguments:
- waves: bfloat16 [32, 192, 192, 192], P('band', 'grid'), may hold values from -6 to 6
- potential: bfloat16 [192, 192, 192], P(None, 'grid'), may hold values from -3 to 1
- block_index: int32 [16384], P('grid'), may hold values from 0 to 1727
- atom_of_slot: int32 [16384], P('grid'), may hold values from 0 to 1023, as said below
- projectors: bfloat16 [16384, 8, 128], P('grid'), may hold values from -0.5 to 0.5
- coupling: float32 [1024, 8, 8], P('grid'), may hold values from -8 to 8
Outputs:
- applied: bfloat16 [32, 192, 192, 192], P('band', 'grid')
Inputs may be any that keep to these rules, and one draw needn't show every extreme that they name: `atom_of_slot`: atom a has its home slab a // 32; the atom of slot s has its home in slab s // 512 or in one of the two slabs beside it, counted cyclically.
All inputs are finite; a program needn't handle non-finite values.
Results may differ from a plain program's by a relative error of at most 0.015.
Values may be sent and summed in bfloat16 or wider, within the bound.
A program may use at most 64 MiB of HBM per device.

v0:
```python
import math

import jax
import jax.numpy as jnp
from jax import lax
from jax.sharding import PartitionSpec as P

BLOCK = 128


def extended(cells, sides, width):
    for axis, dim in sides:
        count = lax.axis_size(axis)
        head = lax.slice_in_dim(cells, 0, width, axis=dim)
        tail = lax.slice_in_dim(cells, cells.shape[dim] - width, cells.shape[dim], axis=dim)
        cells = jnp.concatenate(
            [
                lax.ppermute(tail, axis, [(i, (i + 1) % count) for i in range(count)]),
                cells,
                lax.ppermute(head, axis, [((i + 1) % count, i) for i in range(count)]),
            ],
            axis=dim,
        )
    return cells


def hartley_part(out_index, in_index, size):
    product = out_index[:, None] * in_index[None, :] % size
    angles = 2.0 * math.pi / size * product.astype(jnp.float32)
    return ((jnp.cos(angles) + jnp.sin(angles)) / math.sqrt(size)).astype(jnp.bfloat16)


def folded_squares(counter, size):
    folded = jnp.minimum(counter, size - counter)
    return (folded * folded).astype(jnp.float32)


def shards(waves, potential, block_index, atom_of_slot, projectors, coupling):
    bands_here, thick, size, _ = waves.shape
    groups = lax.axis_size("grid")
    slab_index = lax.axis_index("grid")
    highest = lax.Precision.HIGHEST
    radius = size // 4
    local_x = slab_index * thick + jnp.arange(thick, dtype=jnp.int32)
    full_index = jnp.arange(size, dtype=jnp.int32)
    squares = folded_squares(full_index, size)
    x_squares = folded_squares(local_x, size)
    wave_sq = x_squares[:, None, None] + squares[None, :, None] + squares[None, None, :]
    inside = wave_sq < radius * radius
    kinetic = wave_sq / (radius * radius)
    plane_wave = jnp.where(inside[None], waves, jnp.zeros_like(waves))
    table_in = hartley_part(full_index, full_index, size)
    table_x = hartley_part(full_index, full_index, size)
    table_out = hartley_part(full_index, full_index, size)
    table_back = hartley_part(full_index, full_index, size)
    first = jnp.einsum(
        "bxyz,kz->bxyk", plane_wave, table_in, preferred_element_type=jnp.float32
    ).astype(jnp.bfloat16)
    second = jnp.einsum(
        "bxyz,ky->bxkz", first, table_in, preferred_element_type=jnp.float32
    ).astype(jnp.bfloat16)
    collected = []
    for member in range(bands_here):
        arrived = lax.all_to_all(
            second[member : member + 1], "grid", split_axis=2, concat_axis=1, tiled=True
        )
        collected.append(
            jnp.einsum(
                "kx,bxyz->bkyz", table_x, arrived, preferred_element_type=jnp.float32
            ).astype(jnp.bfloat16)
        )
    real_space = jnp.concatenate(collected, axis=0)
    per_slab = coupling.shape[0]
    blocks = real_space.reshape(bands_here, -1, BLOCK)
    rows = blocks[:, block_index]
    intersection = jnp.einsum("spq,bsq->bsp", projectors, rows, preferred_element_type=jnp.float32)
    home_of = atom_of_slot // per_slab
    relative = (home_of - slab_index + 1 + groups) % groups
    local_atom = relative * per_slab + atom_of_slot % per_slab
    one_hot = (local_atom[:, None] == jnp.arange(3 * per_slab, dtype=jnp.int32)[None, :]).astype(
        jnp.float32
    )
    partial_coef = jnp.einsum("sa,bsp->bap", one_hot, intersection, precision=highest)
    partial_coef = partial_coef.reshape(bands_here, 3, per_slab, -1)
    padded_coef = extended(partial_coef, (("grid", 1),), 1)
    own_coef = padded_coef[:, 0] + padded_coef[:, 2] + padded_coef[:, 4]
    own_coupled = jnp.einsum("apq,baq->bap", coupling, own_coef, precision=highest).astype(
        jnp.bfloat16
    )
    coupled = extended(own_coupled, (("grid", 1),), per_slab)
    selected = jnp.einsum(
        "sa,bap->bsp", one_hot, coupled.astype(jnp.float32), precision=highest
    ).astype(jnp.bfloat16)
    back = jnp.einsum("spq,bsp->bsq", projectors, selected, preferred_element_type=jnp.float32)
    spread_back = jnp.zeros(blocks.shape, jnp.float32).at[:, block_index].add(back)
    mixed = (
        potential.astype(jnp.float32)[None] * real_space.astype(jnp.float32)
        + spread_back.reshape(real_space.shape)
    ).astype(jnp.bfloat16)
    third = jnp.einsum(
        "kx,bxyz->bkyz", table_back, mixed, preferred_element_type=jnp.float32
    ).astype(jnp.bfloat16)
    returned = []
    for member in range(bands_here):
        arrived = lax.all_to_all(
            third[member : member + 1], "grid", split_axis=1, concat_axis=2, tiled=True
        )
        middle = jnp.einsum(
            "bxyz,ky->bxkz", arrived, table_out, preferred_element_type=jnp.float32
        ).astype(jnp.bfloat16)
        returned.append(
            jnp.einsum("bxyz,kz->bxyk", middle, table_out, preferred_element_type=jnp.float32)
        )
    fifth = jnp.concatenate(returned, axis=0)
    total = kinetic[None] * plane_wave.astype(jnp.float32) + fifth
    return jnp.where(inside[None], total, jnp.zeros_like(total)).astype(jnp.bfloat16)


def solution(mesh):
    in_specs = (
        P("band", "grid", None, None),
        P(None, "grid", None),
        P("grid"),
        P("grid"),
        P("grid", None, None),
        P("grid", None, None),
    )
    out_specs = P("band", "grid", None, None)
    return jax.shard_map(shards, mesh=mesh, in_specs=in_specs, out_specs=out_specs, check_vma=False)
```

profile of v0, /device:TPU:1, one launch (start us, length us, event | category | flops | bytes accessed | tf_op | source)
XLA Modules:
  0.0 235.5 jit_solution(12567039091405372556)
XLA Ops:
  0.1 0.3 add_compare_fusion
  0.4 4.1 %fusion.2 = bf16[2,6,192,192]{3,2,1,0:T(8,128)(2,1)} fusion(bf16[2,6,192,192]{3,2,1,0:T(8,128)(2,1)} %param.6, pred[6,192,192]{2,1,0:T(8,128)(4,1)S(1)} %add_compare_fusion), kind=kOutput, calls=%fused_computation.11 | convolution fusion | flops 341950464 | bytes 1990656 | tf_op jit(solution)/shard_map/bxyz,ky->bxkz/dot_general | solution.py:59
  4.5 1.3 fusion.90
  5.8 1.2 copy.32
  7.1 13.0 %all-to-all-start = ((bf16[1,6,192,192]{3,1,0,2:T(8,128)(2,1)}), bf16[1,6,192,192]{3,1,0,2:T(8,128)(2,1)S(1)}, u32[]{:S(2)}, u32[]{:S(2)}) async-start(bf16[1,6,192,192]{3,1,0,2:T(8,128)(2,1)} %copy.32), calls=%async_computation | async-start | bytes 1572864 | tf_op jit(solution)/shard_map/all_to_all | solution.py:64
  20.1 1.2 copy.36
  21.3 20.3 %all-to-all-done = bf16[1,6,192,192]{3,1,0,2:T(8,128)(2,1)S(1)} async-done(((bf16[1,6,192,192]{3,1,0,2:T(8,128)(2,1)}), bf16[1,6,192,192]{3,1,0,2:T(8,128)(2,1)S(1)}, u32[]{:S(2)}, u32[]{:S(2)}) %all-to-all-start) | async-done | bytes 442400 | tf_op jit(solution)/shard_map/all_to_all | solution.py:64
  41.5 5.3 %all-to-all-start.1 = ((bf16[1,6,192,192]{3,1,0,2:T(8,128)(2,1)}), bf16[1,6,192,192]{3,1,0,2:T(8,128)(2,1)S(1)}, u32[]{:S(2)}, u32[]{:S(2)}) async-start(bf16[1,6,192,192]{3,1,0,2:T(8,128)(2,1)} %copy.36), calls=%async_computation.1 | async-start | bytes 1572864 | tf_op jit(solution)/shard_map/all_to_all | solution.py:64
  46.9 0.2 copy.73
  47.1 0.3 copy.34
  47.4 1.2 reshape.104
  48.6 2.2 fusion.4
  50.8 17.5 %all-to-all-done.1 = bf16[1,6,192,192]{3,1,0,2:T(8,128)(2,1)S(1)} async-done(((bf16[1,6,192,192]{3,1,0,2:T(8,128)(2,1)}), bf16[1,6,192,192]{3,1,0,2:T(8,128)(2,1)S(1)}, u32[]{:S(2)}, u32[]{:S(2)}) %all-to-all-start.1) | async-done | bytes 442400 | tf_op jit(solution)/shard_map/all_to_all | solution.py:64
  68.3 0.2 copy.72
  68.5 0.3 copy.38
  68.8 0.4 reshape.105
  69.2 1.1 fusion.5
  70.3 0.8 copy-done.3
  71.1 1.2 pad_maximum_fusion
  72.4 2.5 %copy.40 = bf16[2,192,6,192]{3,2,1,0:T(8,128)(2,1)S(1)} copy(bf16[2,192,6,192]{1,3,2,0:T(8,128)(2,1)} %pad_maximum_fusion) | data formatting | bytes 1769472 | tf_op jit(solution)/shard_map/concatenate | solution.py:72
  74.8 1.6 reshape.106
  76.5 7.3 %copy.41 = bf16[2,1728,128]{2,0,1:T(2,128)(2,1)S(1)} copy(bf16[2,1728,128]{2,1,0:T(8,128)(2,1)S(1)} %reshape.106) | data formatting | bytes 1769472 | tf_op jit(solution)/shard_map/reshape | solution.py:74
  83.8 2.1 gather_fusion
  86.0 0.7 convolution_bitcast_fusion.2
  86.7 0.5 convolution_bitcast_fusion.3
  87.2 0.1 reshape.107
  87.3 4.2 %collective-permute-start = (f32[2,1,32,8]{2,1,3,0:T(1,128)S(1)}, f32[2,1,32,8]{2,1,3,0:T(1,128)S(1)}, u32[]{:S(2)}, u32[]{:S(2)}) collective-permute-start(f32[2,1,32,8]{2,1,3,0:T(1,128)S(1)} %get-tuple-element.9), channel_id=1, source_target_pairs={{0,1},{1,2},{2,3},{3,4},{4,5},{5,6},{6,7},{7,8},{8,9},{9,10},{10,1... | collective-permute-start | bytes 6152 | tf_op jit(solution)/shard_map/ppermute | solution.py:18
  91.6 1.9 collective-permute-start.1
  93.5 0.1 copy.44
  93.6 2.9 %collective-permute-done.1 = f32[2,1,32,8]{2,1,3,0:T(1,128)S(1)} collective-permute-done((f32[2,1,32,8]{2,1,3,0:T(1,128)S(1)}, f32[2,1,32,8]{2,1,3,0:T(1,128)S(1)}, u32[]{:S(2)}, u32[]{:S(2)}) %collective-permute-start.1) | collective-permute-done | bytes 2080 | tf_op jit(solution)/shard_map/ppermute | solution.py:20
  96.6 0.1 copy.43
  96.6 0.3 fusion.9
  97.0 1.9 collective-permute-start.2
  98.9 2.6 %collective-permute-start.3 = (bf16[2,32,8]{2,0,1:T(2,128)(2,1)S(1)}, bf16[2,32,8]{2,0,1:T(2,128)(2,1)S(1)}, u32[]{:S(2)}, u32[]{:S(2)}) collective-permute-start(bf16[2,32,8]{2,0,1:T(2,128)(2,1)S(1)} %fusion.9), channel_id=1, source_target_pairs={{1,0},{2,1},{3,2},{4,3},{5,4},{6,5},{7,6},{8,7},{9,8},{10,9},{11,1... | collective-permute-start | bytes 3080 | tf_op jit(solution)/shard_map/ppermute | solution.py:20
  101.6 0.3 copy.31
  101.8 0.1 copy.46
  101.9 0.1 copy.45
  102.0 2.0 collective-permute-done.3
  104.1 0.2 fusion.10
  104.3 0.2 copy.48
  104.5 0.7 fusion.92
  105.1 1.5 broadcast_in_dim.21
  106.6 49.0 %scatter_fusion = f32[2,1728,128]{2,0,1:T(2,128)} fusion(f32[2,1728,128]{2,0,1:T(2,128)} %broadcast_in_dim.21, s32[512]{0:T(512)S(1)} %compare_select_fusion, f32[512,2,128]{2,1,0:T(2,128)S(1)} %fusion.92), kind=kCustom, calls=%fused_computation.1 | custom fusion | flops 131072 | bytes 1574912 | tf_op jit(solution)/shard_map/scatter-add | solution.py:95
  155.6 2.8 %copy.49 = f32[2,1728,128]{2,1,0:T(8,128)} copy(f32[2,1728,128]{2,0,1:T(2,128)} %scatter_fusion) | data formatting | bytes 3538944 | tf_op jit(solution)/shard_map/scatter-add | solution.py:95
  158.4 3.6 %reshape.108 = f32[2,192,6,192]{3,2,1,0:T(8,128)} reshape(f32[2,1728,128]{2,1,0:T(8,128)} %copy.49) | data formatting | bytes 3538944 | tf_op jit(solution)/shard_map/reshape | solution.py:98
  162.0 3.7 %copy.50 = f32[2,192,6,192]{1,3,2,0:T(8,128)} copy(f32[2,192,6,192]{3,2,1,0:T(8,128)} %reshape.108) | data formatting | bytes 3538944 | tf_op jit(solution)/shard_map/reshape | solution.py:98
  165.7 2.9 %fusion.3 = bf16[2,192,6,192]{1,3,2,0:T(8,128)(2,1)S(1)} fusion(f32[2,192,6,192]{1,3,2,0:T(8,128)} %copy.50, f32[192,6,192]{0,2,1:T(8,128)S(1)} %copy.31, bf16[1,192,6,192]{1,3,2,0:T(8,128)(2,1)S(1)} %copy-done.4, bf16[1,192,6,192]{1,3,2,0:T(8,128)(2,1)S(1)} %copy-done.2), kind=kOutput, calls=%fused_computation.12 | convolution fusion | flops 172965888 | bytes 4423680 | tf_op jit(solution)/shard_map/kx,bxyz->bkyz/dot_general | solution.py:100
  168.7 0.1 fusion.89
  168.8 1.5 copy.54
  170.3 7.1 %all-to-all-start.3 = ((bf16[1,192,6,192]{3,2,0,1:T(8,128)(2,1)}), bf16[1,192,6,192]{3,2,0,1:T(8,128)(2,1)S(1)}, u32[]{:S(2)}, u32[]{:S(2)}) async-start(bf16[1,192,6,192]{3,2,0,1:T(8,128)(2,1)} %copy.54), calls=%async_computation.3 | async-start | bytes 1572864 | tf_op jit(solution)/shard_map/all_to_all | solution.py:105
  177.4 1.5 copy.51
  178.9 19.9 %all-to-all-done.3 = bf16[1,192,6,192]{3,2,0,1:T(8,128)(2,1)S(1)} async-done(((bf16[1,192,6,192]{3,2,0,1:T(8,128)(2,1)}), bf16[1,192,6,192]{3,2,0,1:T(8,128)(2,1)S(1)}, u32[]{:S(2)}, u32[]{:S(2)}) %all-to-all-start.3) | async-done | bytes 442400 | tf_op jit(solution)/shard_map/all_to_all | solution.py:105
  198.9 5.3 %all-to-all-start.2 = ((bf16[1,192,6,192]{3,2,0,1:T(8,128)(2,1)}), bf16[1,192,6,192]{3,2,0,1:T(8,128)(2,1)}, u32[]{:S(2)}, u32[]{:S(2)}) async-start(bf16[1,192,6,192]{3,2,0,1:T(8,128)(2,1)} %copy.51), calls=%async_computation.2 | async-start | bytes 1572864 | tf_op jit(solution)/shard_map/all_to_all | solution.py:105
  204.2 0.2 add_multiply_fusion
  204.4 0.2 copy.70
  204.6 0.3 copy.56
  204.9 1.2 reshape.111
  206.1 3.3 %convolution_bitcast_fusion = f32[1,6,192,192]{3,2,1,0:T(8,128)} fusion(bf16[6,192,192]{2,1,0:T(8,128)(2,1)} %reshape.111), kind=kOutput, calls=%fused_computation.13 | convolution fusion | flops 170975232 | bytes 1327104 | tf_op jit(solution)/shard_map/bxyz,kz->bxyk/dot_general | solution.py:112
  209.4 16.3 %all-to-all-done.2 = bf16[1,192,6,192]{3,2,0,1:T(8,128)(2,1)} async-done(((bf16[1,192,6,192]{3,2,0,1:T(8,128)(2,1)}), bf16[1,192,6,192]{3,2,0,1:T(8,128)(2,1)}, u32[]{:S(2)}, u32[]{:S(2)}) %all-to-all-start.2) | async-done | bytes 442400 | tf_op jit(solution)/shard_map/all_to_all | solution.py:105
  225.8 1.3 copy.71
  227.0 0.3 copy.53
  227.4 1.2 reshape.109
  228.6 3.4 %convolution_bitcast_fusion.1 = f32[1,6,192,192]{3,2,1,0:T(8,128)} fusion(bf16[6,192,192]{2,1,0:T(8,128)(2,1)} %reshape.109), kind=kOutput, calls=%fused_computation.14 | convolution fusion | flops 170975232 | bytes 1327104 | tf_op jit(solution)/shard_map/bxyz,kz->bxyk/dot_general | solution.py:112
  231.9 3.6 %fusion.1 = bf16[2,6,192,192]{3,2,1,0:T(8,128)(2,1)} fusion(f32[1,6,192,192]{3,2,1,0:T(8,128)} %convolution_bitcast_fusion, f32[1,6,192,192]{3,2,1,0:T(8,128)} %convolution_bitcast_fusion.1, f32[6,192,192]{2,1,0:T(8,128)S(1)} %add_multiply_fusion, pred[6,192,192]{2,1,0:T(8,128)(4,1)S(1)} %copy-done.6, bf16[2,6,192,192]{3,2,1,0:T(8,128)(2,1)} %param.6), kind=kLoop, calls=%fused_computation.4 | loop fusion | flops 3096576 | bytes 4644864 | tf_op jit(solution)/shard_map/convert_element_type | solution.py:116
  (32 shorter events, 0.3 us)
Async XLA Ops:
  0.0 85.9 %copy-start = (bf16[512,8,128]{2,1,0:T(8,128)(2,1)S(1)}, bf16[512,8,128]{2,1,0:T(8,128)(2,1)}, u32[]{:S(2)}) copy-start(bf16[512,8,128]{2,1,0:T(8,128)(2,1)} %param.10) | copy-start | bytes 3145732
  0.4 4.1 %copy-start.5 = (pred[6,192,192]{2,1,0:T(8,128)(4,1)}, pred[6,192,192]{2,1,0:T(8,128)(4,1)S(1)}, u32[]{:S(2)}) copy-start(pred[6,192,192]{2,1,0:T(8,128)(4,1)S(1)} %add_compare_fusion) | copy-start | bytes 663556
  7.1 34.5 %all-to-all-start = ((bf16[1,6,192,192]{3,1,0,2:T(8,128)(2,1)}), bf16[1,6,192,192]{3,1,0,2:T(8,128)(2,1)S(1)}, u32[]{:S(2)}, u32[]{:S(2)}) async-start(bf16[1,6,192,192]{3,1,0,2:T(8,128)(2,1)} %copy.32), calls=%async_computation | async-start | bytes 1572864 | tf_op jit(solution)/shard_map/all_to_all | solution.py:64
  20.1 26.8 %copy-start.9 = (s32[512]{0:T(512)S(1)}, s32[512]{0:T(512)}, u32[]{:S(2)}) copy-start(s32[512]{0:T(512)} %param.8) | copy-start | bytes 6148
  20.1 26.8 %copy-start.10 = (s32[512]{0:T(512)S(1)}, s32[512]{0:T(512)}, u32[]{:S(2)}) copy-start(s32[512]{0:T(512)} %param.9) | copy-start | bytes 6148
  41.5 26.8 %all-to-all-start.1 = ((bf16[1,6,192,192]{3,1,0,2:T(8,128)(2,1)}), bf16[1,6,192,192]{3,1,0,2:T(8,128)(2,1)S(1)}, u32[]{:S(2)}, u32[]{:S(2)}) async-start(bf16[1,6,192,192]{3,1,0,2:T(8,128)(2,1)} %copy.36), calls=%async_computation.1 | async-start | bytes 1572864 | tf_op jit(solution)/shard_map/all_to_all | solution.py:64
  50.8 19.5 %copy-start.1 = (bf16[1,192,6,192]{1,3,2,0:T(8,128)(2,1)}, bf16[1,192,6,192]{1,3,2,0:T(8,128)(2,1)S(1)}, u32[]{:S(2)}) copy-start(bf16[1,192,6,192]{1,3,2,0:T(8,128)(2,1)S(1)} %fusion.4) | copy-start | bytes 1327108
  70.3 0.8 copy-start.3
  85.9 7.6 %copy-start.8 = (f32[32,8,8]{0,2,1:T(8,128)S(1)}, f32[32,8,8]{0,2,1:T(8,128)}, u32[]{:S(2)}) copy-start(f32[32,8,8]{0,2,1:T(8,128)} %param.11) | copy-start | bytes 24580
  86.0 15.6 %copy-start.7 = (bf16[192,6,192]{2,0,1:T(8,128)(2,1)S(1)}, bf16[192,6,192]{2,0,1:T(8,128)(2,1)}, u32[]{:S(2)}) copy-start(bf16[192,6,192]{2,0,1:T(8,128)(2,1)} %param.7) | copy-start | bytes 1327108
  87.3 6.3 %collective-permute-start = (f32[2,1,32,8]{2,1,3,0:T(1,128)S(1)}, f32[2,1,32,8]{2,1,3,0:T(1,128)S(1)}, u32[]{:S(2)}, u32[]{:S(2)}) collective-permute-start(f32[2,1,32,8]{2,1,3,0:T(1,128)S(1)} %get-tuple-element.9), channel_id=1, source_target_pairs={{0,1},{1,2},{2,3},{3,4},{4,5},{5,6},{6,7},{7,8},{8,9},{9,10},{10,1... | collective-permute-start | bytes 6152 | tf_op jit(solution)/shard_map/ppermute | solution.py:18
  91.6 5.0 %collective-permute-start.1 = (f32[2,1,32,8]{2,1,3,0:T(1,128)S(1)}, f32[2,1,32,8]{2,1,3,0:T(1,128)S(1)}, u32[]{:S(2)}, u32[]{:S(2)}) collective-permute-start(f32[2,1,32,8]{2,1,3,0:T(1,128)S(1)} %get-tuple-element.10), channel_id=1, source_target_pairs={{1,0},{2,1},{3,2},{4,3},{5,4},{6,5},{7,6},{8,7},{9,8},{10,9},{11,1... | collective-permute-start | bytes 6152 | tf_op jit(solution)/shard_map/ppermute | solution.py:20
  97.0 4.9 %collective-permute-start.2 = (bf16[2,32,8]{2,0,1:T(2,128)(2,1)S(1)}, bf16[2,32,8]{2,0,1:T(2,128)(2,1)S(1)}, u32[]{:S(2)}, u32[]{:S(2)}) collective-permute-start(bf16[2,32,8]{2,0,1:T(2,128)(2,1)S(1)} %fusion.9), channel_id=1, source_target_pairs={{0,1},{1,2},{2,3},{3,4},{4,5},{5,6},{6,7},{7,8},{8,9},{9,10},{10,1... | collective-permute-start | bytes 3080 | tf_op jit(solution)/shard_map/ppermute | solution.py:18
  98.9 5.1 %collective-permute-start.3 = (bf16[2,32,8]{2,0,1:T(2,128)(2,1)S(1)}, bf16[2,32,8]{2,0,1:T(2,128)(2,1)S(1)}, u32[]{:S(2)}, u32[]{:S(2)}) collective-permute-start(bf16[2,32,8]{2,0,1:T(2,128)(2,1)S(1)} %fusion.9), channel_id=1, source_target_pairs={{1,0},{2,1},{3,2},{4,3},{5,4},{6,5},{7,6},{8,7},{9,8},{10,9},{11,1... | collective-permute-start | bytes 3080 | tf_op jit(solution)/shard_map/ppermute | solution.py:20
  162.0 3.7 %copy-start.2 = (bf16[1,192,6,192]{1,3,2,0:T(8,128)(2,1)S(1)}, bf16[1,192,6,192]{1,3,2,0:T(8,128)(2,1)}, u32[]{:S(2)}) copy-start(bf16[1,192,6,192]{1,3,2,0:T(8,128)(2,1)} %copy-done.1) | copy-start | bytes 1327108
  162.0 3.7 %copy-start.4 = (bf16[1,192,6,192]{1,3,2,0:T(8,128)(2,1)S(1)}, bf16[1,192,6,192]{1,3,2,0:T(8,128)(2,1)}, u32[]{:S(2)}) copy-start(bf16[1,192,6,192]{1,3,2,0:T(8,128)(2,1)} %copy-done.3) | copy-start | bytes 1327108
  170.3 28.6 %all-to-all-start.3 = ((bf16[1,192,6,192]{3,2,0,1:T(8,128)(2,1)}), bf16[1,192,6,192]{3,2,0,1:T(8,128)(2,1)S(1)}, u32[]{:S(2)}, u32[]{:S(2)}) async-start(bf16[1,192,6,192]{3,2,0,1:T(8,128)(2,1)} %copy.54), calls=%async_computation.3 | async-start | bytes 1572864 | tf_op jit(solution)/shard_map/all_to_all | solution.py:105
  198.9 26.9 %all-to-all-start.2 = ((bf16[1,192,6,192]{3,2,0,1:T(8,128)(2,1)}), bf16[1,192,6,192]{3,2,0,1:T(8,128)(2,1)}, u32[]{:S(2)}, u32[]{:S(2)}) async-start(bf16[1,192,6,192]{3,2,0,1:T(8,128)(2,1)} %copy.51), calls=%async_computation.2 | async-start | bytes 1572864 | tf_op jit(solution)/shard_map/all_to_all | solution.py:105
  228.6 3.4 %copy-start.6 = (pred[6,192,192]{2,1,0:T(8,128)(4,1)S(1)}, pred[6,192,192]{2,1,0:T(8,128)(4,1)}, u32[]{:S(2)}) copy-start(pred[6,192,192]{2,1,0:T(8,128)(4,1)} %copy-done.5) | copy-start | bytes 663556
where the time goes:
time: 237 us; the launch traced here: 236 us
  waiting for transfers between devices  78.9 us (33%)
  other arithmetic  54.4 us (23%)
  starting transfers between devices  41.4 us (17%)
  local copies, waits for them, and re-layouts  40.9 us (17%)
  matrix products  19.5 us (8%)
    scatter-add x1, other arithmetic, shards(): jnp.zeros(blocks.shape, jnp.float32).at[:, block_index].add(back)  49 us
    all_to_all x2, waiting for transfers between devices, shards(): lax.all_to_all(second[member:member + 1], 'grid', split_axis=2, concat_ax...  37.8 us
    all_to_all x2, waiting for transfers between devices, shards(): lax.all_to_all(third[member:member + 1], 'grid', split_axis=1, concat_axi...  36.2 us
    all_to_all x2, starting transfers between devices, shards(): lax.all_to_all(second[member:member + 1], 'grid', split_axis=2, concat_ax...  18.3 us
    all_to_all x2, starting transfers between devices, shards(): lax.all_to_all(third[member:member + 1], 'grid', split_axis=1, concat_axi...  12.4 us
    reshape x2, local copies, waits for them, and re-layouts, shards(): blocks = real_space.reshape(bands_here, -1, BLOCK)  8.96 us
    reshape x2, local copies, waits for them, and re-layouts, shards(): spread_back.reshape(real_space.shape)  7.3 us
    dot_general x2, matrix products, shards(): jnp.einsum('bxyz,kz->bxyk', middle, table_out, preferred_element_type=jnp...  6.71 us
  transfers between devices with their start and end apart: 8, of which 6 were waited for; matrix products, arithmetic and copies ran while one was open for 5% of the time, Pallas kernels for 0%

commit v1 on v0

v1 whole, which is shorter than its diff:
```python
import functools
import math

import jax
import jax.numpy as jnp
import ml_dtypes
import numpy as np
from jax import lax
from jax.experimental import pallas as pl
from jax.experimental.pallas import tpu as pltpu
from jax.sharding import PartitionSpec as P

MESH = pl.DeviceIdType.MESH
F32, BF16 = jnp.float32, jnp.bfloat16
N, G, T = 192, 32, 6
A = 16
RAD2 = 48 * 48
KEEP = np.concatenate([np.arange(48), np.arange(144, 192)])
OFFSETS = (1, -1, 2, -2)


def tables():
    k = np.arange(N)
    angles = np.float32(2.0 * math.pi / N) * ((k[:, None] * k[None, :]) % N).astype(np.float32)
    c = ((np.cos(angles) + np.sin(angles)) / np.float32(math.sqrt(N))).astype(ml_dtypes.bfloat16)
    c = c.astype(np.float32)
    cy = np.zeros((G, 2, 8, 2, 96), np.float32)
    for par in range(2):
        cy[:, par, :T, par, :] = c[:, KEEP].reshape(G, T, 96)
    cy = cy.reshape(512, 192)
    lx = np.zeros((T, N, 96, 8), np.float32)
    for y in range(T):
        lx[y, :, :, y] = c[:, KEEP]
    lx = lx.reshape(T * N, 768)
    lane = np.arange(128)
    kz = np.where(lane < 64, lane, lane + 64)
    half = c[kz, :] * ((lane < 48) | (lane >= 80))[:, None]
    wz = np.zeros((2, 128, 2, N), np.float32)
    wz[0, :, 0, :] = half
    wz[1, :, 1, :] = half
    wz = wz.reshape(256, 384)
    out = [cy, np.ascontiguousarray(cy.T), lx, np.ascontiguousarray(lx.T), wz, np.ascontiguousarray(wz.T)]
    return [x.astype(ml_dtypes.bfloat16) for x in out]


def dot(a, b):
    return jnp.dot(a, b, preferred_element_type=F32)


def folded_sq(k):
    f = jnp.minimum(k, N - k)
    return f * f


def sphere_sq(kx):
    row = lax.broadcasted_iota(jnp.int32, (96, 128), 0)
    lane = lax.broadcasted_iota(jnp.int32, (96, 128), 1)
    ky = jnp.where(row < 48, row, row + 96)
    kz = jnp.where(lane < 64, lane, lane + 64)
    return folded_sq(kx) + folded_sq(ky) + folded_sq(kz)


def squeeze_z(w):
    return jnp.concatenate([w[:, :64], w[:, 128:]], axis=1)


def main_kernel(
    waves, pot, idx_ref, atom_ref, proj, coup_ref, cy, lx, lxt, wz_ref, wzt_ref, out,
    wlo, whi, cyv, lxv, lxtv, potv, projv, projt, potc, oh1, oh2, oha, exp_up,
    send1, recv1, xbuf, rs, mx, send2, coef_out, coef_in, coup_in,
    load_sem, s1, r1, s2, r2, self_sem, cs, cr, ks, kr,
):
    g = lax.axis_index("grid")
    active = jnp.logical_or(g < 8, g >= 24)
    ai = jnp.where(g < 8, g, g - 16)

    def peer(d):
        return lax.rem(g + d + G, G)

    loads = [
        pltpu.make_async_copy(lx, lxv, load_sem.at[0]),
        pltpu.make_async_copy(lxt, lxtv, load_sem.at[1]),
        pltpu.make_async_copy(pot, potv, load_sem.at[2]),
        pltpu.make_async_copy(proj, projv, load_sem.at[3]),
    ]
    wave_loads = [
        pltpu.make_async_copy(waves.at[:, :, 0:48, :], wlo, load_sem.at[4]),
        pltpu.make_async_copy(waves.at[:, :, 144:192, :], whi, load_sem.at[5]),
        pltpu.make_async_copy(cy, cyv, load_sem.at[6]),
    ]

    @pl.when(active)
    def _():
        for copy in wave_loads:
            copy.start()

    for copy in loads:
        copy.start()

    barrier = pltpu.get_barrier_semaphore()

    def greet(d, carry):
        pl.semaphore_signal(barrier, inc=1, device_id={"grid": peer(d)}, device_id_type=MESH)
        return carry

    lax.fori_loop(1, G, greet, 0)

    @pl.when(active)
    def _():
        for copy in wave_loads:
            copy.wait()
        for kp in range(3):
            parts = []
            for par in range(2):
                kx = g * T + 2 * kp + par
                inside = sphere_sq(kx) < RAD2
                cols = []
                for b in range(2):
                    w = jnp.concatenate([wlo[b, 2 * kp + par], whi[b, 2 * kp + par]], axis=0)
                    w = squeeze_z(w.astype(F32))
                    cols.append(jnp.where(inside, w, 0.0).astype(BF16))
                parts.append(jnp.concatenate(cols, axis=1))
            rhs = jnp.concatenate(parts, axis=0)
            send1[:, kp] = dot(cyv[...], rhs).astype(BF16).reshape(G, 16, 256)

    pl.semaphore_wait(barrier, G - 1)

    def first_copy(d):
        to = peer(d)
        return pltpu.make_async_remote_copy(
            src_ref=send1.at[to], dst_ref=recv1.at[ai], send_sem=s1.at[d], recv_sem=r1.at[ai],
            device_id={"grid": to}, device_id_type=MESH,
        )

    @pl.when(active)
    def _():
        def go(d, carry):
            first_copy(d).start()
            return carry

        lax.fori_loop(1, G, go, 0)
        recv1[ai] = send1[g]

    coup_copies = [
        pltpu.make_async_remote_copy(
            src_ref=coup_ref, dst_ref=coup_in.at[n], send_sem=ks.at[n], recv_sem=kr.at[n],
            device_id={"grid": peer(d)}, device_id_type=MESH,
        )
        for n, d in enumerate(OFFSETS[:2])
    ]
    for copy in coup_copies:
        copy.start()

    idx_row = idx_ref[...]
    atom_row = atom_ref[...]
    atom_row = ((lax.shift_right_logical(atom_row, 5) - g + 33) & 31) * 32 + (atom_row & 31)

    def column(row):
        return jnp.transpose(jnp.broadcast_to(row.astype(F32), (128, 512))).astype(jnp.int32)

    idx_col = column(idx_row)
    idx_col = jnp.concatenate([idx_col, idx_col[:, :64]], axis=1)
    lane192 = lax.broadcasted_iota(jnp.int32, (512, N), 1) * 9
    row192 = lax.broadcasted_iota(jnp.int32, (N, 512), 0) * 9
    for c in range(9):
        oh1[c] = jnp.where(lane192 + c == idx_col, 1.0, 0.0).astype(BF16)
        oh2[c] = jnp.where(row192 + c == idx_row, 1.0, 0.0).astype(BF16)
    lane128 = lax.broadcasted_iota(jnp.int32, (512, 128), 1)
    oha[...] = jnp.where(column(atom_row) == lane128, 1.0, 0.0).astype(BF16)
    up_row = lax.broadcasted_iota(jnp.int32, (128, 2048), 0)
    up_lane = lax.broadcasted_iota(jnp.int32, (128, 2048), 1)
    exp_up[...] = jnp.where(lax.shift_right_logical(up_lane, 7) == up_row, 1.0, 0.0).astype(BF16)
    for copy in loads:
        copy.wait()
    projt[...] = jnp.swapaxes(projv[...].astype(F32), 0, 1)
    pt = jnp.swapaxes(potv[...].astype(F32), 0, 1)
    for j in range(3):
        e, o = pt[2 * j], pt[2 * j + 1]
        potc[3 * j] = e[:, :128]
        potc[3 * j + 1] = jnp.concatenate([e[:, 128:], o[:, :64]], axis=1)
        potc[3 * j + 2] = o[:, 64:]

    def wait_first(i, carry):
        src = jnp.where(i < 8, i, i + 16)

        @pl.when(src != g)
        def _():
            pltpu.make_async_remote_copy(
                src_ref=send1.at[0], dst_ref=recv1.at[i], send_sem=s1.at[0], recv_sem=r1.at[i],
                device_id={"grid": src}, device_id_type=MESH,
            ).wait_recv()

        return carry

    lax.fori_loop(0, A, wait_first, 0)

    for y in range(T):
        xbuf[y] = dot(lxv[y * N : (y + 1) * N, :], recv1[...].reshape(768, 256)).astype(BF16)
    for j in range(3):
        for b in range(2):
            cut = slice(b * 128, (b + 1) * 128)
            eo = jnp.concatenate([xbuf[2 * j, :, cut], xbuf[2 * j + 1, :, cut]], axis=1)
            real = dot(eo, wz_ref[...]).astype(BF16)
            for t in range(3):
                rs[3 * j + t, :, cut] = real[:, t * 128 : (t + 1) * 128]

    rows = dot(oh1[0], rs[0])
    for c in range(1, 9):
        rows = rows + dot(oh1[c], rs[c])
    inter = None
    for b in range(2):
        prod = jnp.concatenate(
            [(projt[p] * rows[:, b * 128 : (b + 1) * 128]).astype(BF16) for p in range(8)], axis=1
        )
        term = lax.dot_general(
            prod, exp_up[:, b * 1024 : (b + 1) * 1024], (((1,), (1,)), ((), ())), preferred_element_type=F32
        )
        inter = term if inter is None else inter + term
    inter_t = jnp.transpose(inter)[:16]
    high = inter_t.astype(BF16)
    low = (inter_t - high.astype(F32)).astype(BF16)
    coef_out[...] = dot(high, oha[...]) + dot(low, oha[...])
    coef_copies = [
        pltpu.make_async_remote_copy(
            src_ref=coef_out, dst_ref=coef_in.at[n], send_sem=cs.at[n], recv_sem=cr.at[n],
            device_id={"grid": peer(d)}, device_id_type=MESH,
        )
        for n, d in enumerate(OFFSETS)
    ]
    for copy in coef_copies:
        copy.start()
    for copy in coup_copies:
        copy.wait()
    coup = coup_in[0] + pltpu.roll(coup_ref[...], 32, 1) + pltpu.roll(coup_in[1], 64, 1)
    for copy in coef_copies:
        copy.wait()
    lane16 = lax.broadcasted_iota(jnp.int32, (16, 128), 1)
    coef = coef_out[...] + pltpu.roll(coef_in[0], 96, 1) + pltpu.roll(coef_in[1], 32, 1)
    coef = coef + jnp.where(lane16 < 32, pltpu.roll(coef_in[2], 64, 1), 0.0)
    coef = coef + jnp.where(
        jnp.logical_and(lane16 >= 64, lane16 < 96), pltpu.roll(coef_in[3], 64, 1), 0.0
    )
    mixed_rows = []
    for b in range(2):
        for p in range(8):
            mixed_rows.append(
                jnp.sum(coup[8 * p : 8 * p + 8] * coef[8 * b : 8 * b + 8], axis=0, keepdims=True)
            )
    coupled = jnp.concatenate(mixed_rows, axis=0).astype(BF16)
    coupled = jnp.concatenate([coupled, jnp.zeros((112, 128), BF16)], axis=0)
    chosen = lax.dot_general(
        oha[...], coupled, (((1,), (1,)), ((), ())), preferred_element_type=F32
    ).astype(BF16)
    backs = []
    for b in range(2):
        back = None
        for p in range(8):
            n = (b * 8 + p) * 128
            term = projt[p] * dot(chosen, exp_up[:, n : n + 128])
            back = term if back is None else back + term
        backs.append(back)
    back = jnp.concatenate(backs, axis=1)
    high = back.astype(BF16)
    low = (back - high.astype(F32)).astype(BF16)

    for c in range(9):
        spread = dot(oh2[c], high) + dot(oh2[c], low)
        local = potc[c]
        local = jnp.concatenate([local, local], axis=1)
        mx[c] = (local * rs[c].astype(F32) + spread).astype(BF16)
    for j in range(3):
        for b in range(2):
            cut = slice(b * 128, (b + 1) * 128)
            row = jnp.concatenate([mx[3 * j + t, :, cut] for t in range(3)], axis=1)
            eo = dot(row, wzt_ref[...]).astype(BF16)
            xbuf[2 * j, :, cut] = eo[:, :128]
            xbuf[2 * j + 1, :, cut] = eo[:, 128:]
    xall = xbuf[...].reshape(T * N, 256)
    for n in range(4):
        send2[4 * n : 4 * n + 4] = (
            dot(lxtv[n * N : (n + 1) * N, :], xall).astype(BF16).reshape(4, 3, 16, 256)
        )

    def second_copy(i):
        to = jnp.where(i < 8, i, i + 16)
        return to, pltpu.make_async_remote_copy(
            src_ref=send2.at[i], dst_ref=out.at[g], send_sem=s2.at[i], recv_sem=r2.at[g],
            device_id={"grid": to}, device_id_type=MESH,
        )

    def go_back(n, carry):
        i = lax.rem(n + g, A)
        to, copy = second_copy(i)

        @pl.when(to != g)
        def _():
            copy.start()

        return carry

    lax.fori_loop(0, A, go_back, 0)

    @pl.when(active)
    def _():
        own = pltpu.make_async_copy(send2.at[ai], out.at[g], self_sem)
        own.start()
        own.wait()

        def wait_sent(d, carry):
            first_copy(d).wait_send()
            return carry

        lax.fori_loop(1, G, wait_sent, 0)

        def wait_second(src, carry):
            @pl.when(src != g)
            def _():
                pltpu.make_async_remote_copy(
                    src_ref=send2.at[0], dst_ref=out.at[src], send_sem=s2.at[0], recv_sem=r2.at[src],
                    device_id={"grid": src}, device_id_type=MESH,
                ).wait_recv()

            return carry

        lax.fori_loop(0, G, wait_second, 0)

    def wait_back(i, carry):
        to, copy = second_copy(i)

        @pl.when(to != g)
        def _():
            copy.wait_send()

        return carry

    lax.fori_loop(0, A, wait_back, 0)


def last_kernel(cyi, recv, waves, out):
    kp = pl.program_id(0)
    g = lax.axis_index("grid")
    active = jnp.logical_or(g < 8, g >= 24)

    @pl.when(active)
    def _():
        f = dot(cyi[...], recv[...].reshape(512, 256))
        for par in range(2):
            ksq = sphere_sq(g * T + 2 * kp + par)
            inside = ksq < RAD2
            kinetic = ksq.astype(F32) / RAD2
            for b in range(2):
                w = jnp.concatenate([waves[b, par, 0:48, :], waves[b, par, 144:192, :]], axis=0)
                w = squeeze_z(w.astype(F32))
                part = f[par * 96 : (par + 1) * 96, b * 128 : (b + 1) * 128]
                total = jnp.where(inside, kinetic * w + part, 0.0)
                wide = jnp.concatenate([total[:, :64], jnp.zeros((96, 64), F32), total[:, 64:]], axis=1)
                wide = wide.astype(BF16)
                out[b, par, 0:48, :] = wide[:48]
                out[b, par, 48:144, :] = jnp.zeros((96, N), BF16)
                out[b, par, 144:192, :] = wide[48:]

    @pl.when(jnp.logical_not(active))
    def _():
        out[...] = jnp.zeros(out.shape, BF16)


def shards(waves, potential, block_index, atom_of_slot, projectors, coupling):
    cy, cyi, lx, lxt, wz, wzt = (jnp.asarray(x) for x in tables())
    coup = jnp.transpose(coupling, (1, 2, 0)).reshape(64, 32)
    coup = jnp.pad(coup, ((0, 0), (0, 96)))
    any_spec = pl.BlockSpec(memory_space=pl.ANY)
    vmem = pl.BlockSpec(memory_space=pltpu.VMEM)
    dma = pltpu.SemaphoreType.DMA
    recv = pl.pallas_call(
        main_kernel,
        name="exchange_and_apply",
        out_shape=jax.ShapeDtypeStruct((G, 3, 16, 256), BF16),
        in_specs=[any_spec, any_spec, vmem, vmem, any_spec, vmem, any_spec, any_spec, any_spec, vmem, vmem],
        out_specs=any_spec,
        scratch_shapes=[
            pltpu.VMEM((2, T, 48, N), BF16),
            pltpu.VMEM((2, T, 48, N), BF16),
            pltpu.VMEM((512, 192), BF16),
            pltpu.VMEM((T * N, 768), BF16),
            pltpu.VMEM((768, T * N), BF16),
            pltpu.VMEM((N, T, N), BF16),
            pltpu.VMEM((512, 8, 128), BF16),
            pltpu.VMEM((8, 512, 128), F32),
            pltpu.VMEM((9, N, 128), F32),
            pltpu.VMEM((9, 512, N), BF16),
            pltpu.VMEM((9, N, 512), BF16),
            pltpu.VMEM((512, 128), BF16),
            pltpu.VMEM((128, 2048), BF16),
            pltpu.VMEM((G, 3, 16, 256), BF16),
            pltpu.VMEM((A, 3, 16, 256), BF16),
            pltpu.VMEM((T, N, 256), BF16),
            pltpu.VMEM((9, N, 256), BF16),
            pltpu.VMEM((9, N, 256), BF16),
            pltpu.VMEM((A, 3, 16, 256), BF16),
            pltpu.VMEM((16, 128), F32),
            pltpu.VMEM((4, 16, 128), F32),
            pltpu.VMEM((2, 64, 128), F32),
            dma((7,)),
            dma((G,)),
            dma((A,)),
            dma((A,)),
            dma((G,)),
            dma,
            dma((4,)),
            dma((4,)),
            dma((2,)),
            dma((2,)),
        ],
        compiler_params=pltpu.CompilerParams(
            collective_id=0, has_side_effects=True, vmem_limit_bytes=48 << 20
        ),
    )(
        waves, potential, block_index.reshape(1, -1), atom_of_slot.reshape(1, -1), projectors, coup,
        cy, lx, lxt, wz, wzt,
    )
    return pl.pallas_call(
        last_kernel,
        name="finish",
        grid=(3,),
        out_shape=jax.ShapeDtypeStruct(waves.shape, BF16),
        in_specs=[
            pl.BlockSpec((192, 512), lambda k: (0, 0)),
            pl.BlockSpec((G, 1, 16, 256), lambda k: (0, k, 0, 0)),
            pl.BlockSpec((2, 2, N, N), lambda k: (0, k, 0, 0)),
        ],
        out_specs=pl.BlockSpec((2, 2, N, N), lambda k: (0, k, 0, 0)),
        compiler_params=pltpu.CompilerParams(vmem_limit_bytes=32 << 20),
    )(cyi, recv, waves)


def solution(mesh):
    in_specs = (
        P("band", "grid", None, None),
        P(None, "grid", None),
        P("grid"),
        P("grid"),
        P("grid", None, None),
        P("grid", None, None),
    )
    out_specs = P("band", "grid", None, None)
    return jax.shard_map(shards, mesh=mesh, in_specs=in_specs, out_specs=out_specs, check_vma=False)
```

time: 237 us -> 64.1 us (0.27)
  waiting for transfers between devices: 78.9 us -> 0 us
  Pallas kernels: 0 us -> 56.1 us
  other arithmetic: 54.4 us -> 0 us
  starting transfers between devices: 41.4 us -> 0 us
  local copies, waits for them, and re-layouts: 40.9 us -> 7.65 us
  matrix products: 19.5 us -> 0 us
    all_to_all x4 -> x0, waiting for transfers between devices: 74 us -> none  [the longest x2 37.8 us: shards(): lax.all_to_all(second[member:member + 1], 'grid', split_axis=2, concat_ax...]
    pallas_call x0 -> x2, Pallas kernels: none -> 56.1 us  [the longest x1 53.8 us: shards(): pl.pallas_call(main_kernel, name='exchange_and_apply', out_shape=jax.Shap...]
    scatter-add x1 -> x0, other arithmetic: 49 us -> none  [shards(): jnp.zeros(blocks.shape, jnp.float32).at[:, block_index].add(back)]
    all_to_all x4 -> x0, starting transfers between devices: 30.7 us -> none  [the longest x2 18.3 us: shards(): lax.all_to_all(second[member:member + 1], 'grid', split_axis=2, concat_ax...]
    dot_general x11 -> x0, matrix products: 19.5 us -> none  [the longest x2 6.71 us: shards(): jnp.einsum('bxyz,kz->bxyk', middle, table_out, preferred_element_type=jnp...]
    reshape x5 -> x0, local copies, waits for them, and re-layouts: 16.3 us -> none  [the longest x2 8.96 us: shards(): blocks = real_space.reshape(bands_here, -1, BLOCK)]
    ppermute x4 -> x0, starting transfers between devices: 10.7 us -> none  [the longest x2 6.18 us: extended(): lax.ppermute(tail, axis, [(i, (i + 1) % count) for i in range(count)])]
    slice x7 -> x0, local copies, waits for them, and re-layouts: 6.95 us -> none  [the longest x3 3.76 us: shards(): second[member:member + 1]]
  transfers between devices with their start and end apart: 8 -> 0, of which waited for: 6 -> 0; matrix products, arithmetic and copies ran while one was open for 5% -> 0% of each run, Pallas kernels for 0% -> 0%
where the time goes in v1:
time: 64.1 us; the launch traced here: 63.8 us
  Pallas kernels  56.1 us (88%)
  local copies, waits for them, and re-layouts  7.65 us (12%)
    pallas_call x1, Pallas kernels, shards(): pl.pallas_call(main_kernel, name='exchange_and_apply', out_shape=jax.Shap...  53.8 us
    unnamed x17, local copies, waits for them, and re-layouts  6.79 us
    pallas_call x1, Pallas kernels, shards(): pl.pallas_call(last_kernel, name='finish', grid=(3,), out_shape=jax.Shape...  2.21 us

profile of v1, /device:TPU:1, one launch (start us, length us, event | category | flops | bytes accessed | tf_op | source)
XLA Modules:
  0.0 63.8 jit_solution(2014252203009033194)
XLA Ops:
  0.0 0.0 copy-start
  0.0 0.9 %pad.4.coup_ref = f32[64,128]{1,0:T(8,128)S(1)} pad(f32[64,32]{1,0:T(8,128)} %bitcast.7, f32[]{:T(128)} %constant.14.clone.1), padding=0_0x0_96 | pad | bytes 40964 | tf_op jit(solution)/shard_map/jit(_pad)/pad | solution.py:370
  0.9 1.4 %copy.13.pot = bf16[192,6,192]{2,1,0:T(8,128)(2,1)S(1)} copy(bf16[192,6,192]{2,0,1:T(8,128)(2,1)} %param.13) | data formatting | bytes 884736 | tf_op args[1]
  2.3 0.0 copy-done
  2.3 0.0 copy-start.1
  2.3 1.2 %copy-done.1 = bf16[512,8,128]{2,1,0:T(8,128)(2,1)S(1)} copy-done((bf16[512,8,128]{2,1,0:T(8,128)(2,1)S(1)}, bf16[512,8,128]{2,1,0:T(8,128)(2,1)}, u32[]{:S(2)}) %copy-start.1) | copy-done | bytes 1048600
  3.5 0.0 copy-start.2
  3.5 0.9 %copy-done.2 = bf16[512,192]{1,0:T(8,128)(2,1)S(1)} copy-done((bf16[512,192]{1,0:T(8,128)(2,1)S(1)}, bf16[512,192]{1,0:T(8,128)(2,1)}, u32[]{:S(2)}) %copy-start.2) | copy-done | bytes 196632
  4.5 0.0 copy-start.4
  4.5 0.9 %copy-done.4 = bf16[384,256]{1,0:T(8,128)(2,1)S(1)} copy-done((bf16[384,256]{1,0:T(8,128)(2,1)S(1)}, bf16[384,256]{1,0:T(8,128)(2,1)}, u32[]{:S(2)}) %copy-start.4) | copy-done | bytes 196632
  5.4 0.0 copy-start.5
  5.4 0.9 %copy-done.5 = bf16[256,384]{1,0:T(8,128)(2,1)S(1)} copy-done((bf16[256,384]{1,0:T(8,128)(2,1)S(1)}, bf16[256,384]{1,0:T(8,128)(2,1)}, u32[]{:S(2)}) %copy-start.5) | copy-done | bytes 196632
  6.3 0.0 copy-start.6
  6.3 0.7 %copy-done.6 = s32[512]{0:T(512)S(1)} copy-done((s32[512]{0:T(512)S(1)}, s32[512]{0:T(512)}, u32[]{:S(2)}) %copy-start.6) | copy-done | bytes 2072
  7.0 0.0 copy-start.7
  7.0 0.7 %copy-done.7 = s32[512]{0:T(512)S(1)} copy-done((s32[512]{0:T(512)S(1)}, s32[512]{0:T(512)}, u32[]{:S(2)}) %copy-start.7) | copy-done | bytes 2072
  7.7 0.0 copy-start.3
  7.7 53.8 %exchange_and_apply.1.recv = bf16[32,3,16,256]{3,2,1,0:T(8,128)(2,1)S(1)} custom-call(bf16[2,6,192,192]{3,2,1,0:T(8,128)(2,1)S(1)} %copy-done, bf16[192,6,192]{2,1,0:T(8,128)(2,1)S(1)} %copy.13.pot, s32[1,512]{1,0:T(1,128)S(1)} %bitcast.5, s32[1,512]{1,0:T(1,128)S(1)} %bitcast.6, bf16[512,8,128]{2,1,0:T(8,128)(2,1)S(1)} %copy-done.1, ...), custom_call_target="tpu_custom_call" | custom-call | tf_op jit(solution)/shard_map/exchange_and_apply/pallas_call | solution.py:374
  61.5 0.0 copy-done.3
  61.5 2.2 %finish.1 = bf16[2,6,192,192]{3,2,1,0:T(8,128)(2,1)} custom-call(bf16[192,512]{1,0:T(8,128)(2,1)S(1)} %copy-done.3, bf16[32,3,16,256]{3,2,1,0:T(8,128)(2,1)S(1)} %exchange_and_apply.1.recv, bf16[2,6,192,192]{3,2,1,0:T(8,128)(2,1)S(1)} %copy-done), custom_call_target="tpu_custom_call" | custom-call | tf_op jit(solution)/shard_map/finish/pallas_call | solution.py:421
Async XLA Ops:
  0.0 2.3 %copy-start = (bf16[2,6,192,192]{3,2,1,0:T(8,128)(2,1)S(1)}, bf16[2,6,192,192]{3,2,1,0:T(8,128)(2,1)}, u32[]{:S(2)}) copy-start(bf16[2,6,192,192]{3,2,1,0:T(8,128)(2,1)} %waves.3) | copy-start | bytes 2654212
  2.3 1.2 %copy-start.1 = (bf16[512,8,128]{2,1,0:T(8,128)(2,1)S(1)}, bf16[512,8,128]{2,1,0:T(8,128)(2,1)}, u32[]{:S(2)}) copy-start(bf16[512,8,128]{2,1,0:T(8,128)(2,1)} %proj.1) | copy-start | bytes 3145732
  3.5 0.9 %copy-start.2 = (bf16[512,192]{1,0:T(8,128)(2,1)S(1)}, bf16[512,192]{1,0:T(8,128)(2,1)}, u32[]{:S(2)}) copy-start(bf16[512,192]{1,0:T(8,128)(2,1)} %constant.15.clone.cy) | copy-start | bytes 589828
  4.5 0.9 %copy-start.4 = (bf16[384,256]{1,0:T(8,128)(2,1)S(1)}, bf16[384,256]{1,0:T(8,128)(2,1)}, u32[]{:S(2)}) copy-start(bf16[384,256]{1,0:T(8,128)(2,1)} %constant.20.clone.wzt_ref) | copy-start | bytes 589828
  5.4 0.9 %copy-start.5 = (bf16[256,384]{1,0:T(8,128)(2,1)S(1)}, bf16[256,384]{1,0:T(8,128)(2,1)}, u32[]{:S(2)}) copy-start(bf16[256,384]{1,0:T(8,128)(2,1)} %constant.19.clone.wz_ref) | copy-start | bytes 589828
  6.3 0.7 %copy-start.6 = (s32[512]{0:T(512)S(1)}, s32[512]{0:T(512)}, u32[]{:S(2)}) copy-start(s32[512]{0:T(512)} %param.14) | copy-start | bytes 6148
  7.0 0.7 %copy-start.7 = (s32[512]{0:T(512)S(1)}, s32[512]{0:T(512)}, u32[]{:S(2)}) copy-start(s32[512]{0:T(512)} %param.15) | copy-start | bytes 6148
  7.7 53.9 %copy-start.3 = (bf16[192,512]{1,0:T(8,128)(2,1)S(1)}, bf16[192,512]{1,0:T(8,128)(2,1)}, u32[]{:S(2)}) copy-start(bf16[192,512]{1,0:T(8,128)(2,1)} %constant.16.clone.cyi) | copy-start | bytes 589828

commit v2 on v1

--- a/solution.py
+++ b/solution.py
@@ -28,10 +28,7 @@
     for par in range(2):
         cy[:, par, :T, par, :] = c[:, KEEP].reshape(G, T, 96)
     cy = cy.reshape(512, 192)
-    lx = np.zeros((T, N, 96, 8), np.float32)
-    for y in range(T):
-        lx[y, :, :, y] = c[:, KEEP]
-    lx = lx.reshape(T * N, 768)
+    cx = c[:, KEEP]
     lane = np.arange(128)
     kz = np.where(lane < 64, lane, lane + 64)
     half = c[kz, :] * ((lane < 48) | (lane >= 80))[:, None]
@@ -39,8 +36,8 @@
     wz[0, :, 0, :] = half
     wz[1, :, 1, :] = half
     wz = wz.reshape(256, 384)
-    out = [cy, np.ascontiguousarray(cy.T), lx, np.ascontiguousarray(lx.T), wz, np.ascontiguousarray(wz.T)]
-    return [x.astype(ml_dtypes.bfloat16) for x in out]
+    out = [cy, cy.T, cx, cx.T, wz, wz.T]
+    return [np.ascontiguousarray(x).astype(ml_dtypes.bfloat16) for x in out]
 
 
 def dot(a, b):
@@ -65,9 +62,10 @@
 
 
 def main_kernel(
-    waves, pot, idx_ref, atom_ref, proj, coup_ref, cy, lx, lxt, wz_ref, wzt_ref, out,
-    wlo, whi, cyv, lxv, lxtv, potv, projv, projt, potc, oh1, oh2, oha, exp_up,
-    send1, recv1, xbuf, rs, mx, send2, coef_out, coef_in, coup_in,
+    waves, pot, idx, atom, proj, coup, cy, cx, cxt, wz, wzt, out,
+    wlo, whi, cyv, cxv, cxtv, wzv, wztv, potv, idxv, atomv, projv, coupv,
+    projt, potc, oh1, oh2, oha, exp_up,
+    send1, recv1, xbuf, rs, mx, send2, coup_out, coup_in, coef_out, coef_in,
     load_sem, s1, r1, s2, r2, self_sem, cs, cr, ks, kr,
 ):
     g = lax.axis_index("grid")
@@ -77,17 +75,16 @@
     def peer(d):
         return lax.rem(g + d + G, G)
 
-    loads = [
-        pltpu.make_async_copy(lx, lxv, load_sem.at[0]),
-        pltpu.make_async_copy(lxt, lxtv, load_sem.at[1]),
-        pltpu.make_async_copy(pot, potv, load_sem.at[2]),
-        pltpu.make_async_copy(proj, projv, load_sem.at[3]),
+    wave_loads = [
+        pltpu.make_async_copy(waves.at[:, :, 0:48, :], wlo, load_sem.at[0]),
+        pltpu.make_async_copy(waves.at[:, :, 144:192, :], whi, load_sem.at[1]),
+        pltpu.make_async_copy(cy, cyv, load_sem.at[2]),
     ]
-    wave_loads = [
-        pltpu.make_async_copy(waves.at[:, :, 0:48, :], wlo, load_sem.at[4]),
-        pltpu.make_async_copy(waves.at[:, :, 144:192, :], whi, load_sem.at[5]),
-        pltpu.make_async_copy(cy, cyv, load_sem.at[6]),
-    ]
+    pairs = (
+        (coup, coupv), (idx, idxv), (atom, atomv), (proj, projv), (pot, potv),
+        (cx, cxv), (wz, wzv), (wzt, wztv), (cxt, cxtv),
+    )
+    loads = [pltpu.make_async_copy(a, b, load_sem.at[3 + n]) for n, (a, b) in enumerate(pairs)]
 
     @pl.when(active)
     def _():
@@ -141,9 +138,12 @@
         lax.fori_loop(1, G, go, 0)
         recv1[ai] = send1[g]
 
+    for copy in loads:
+        copy.wait()
+    coup_out[...] = jnp.concatenate([coupv[...], jnp.zeros((64, 96), F32)], axis=1)
     coup_copies = [
         pltpu.make_async_remote_copy(
-            src_ref=coup_ref, dst_ref=coup_in.at[n], send_sem=ks.at[n], recv_sem=kr.at[n],
+            src_ref=coup_out, dst_ref=coup_in.at[n], send_sem=ks.at[n], recv_sem=kr.at[n],
             device_id={"grid": peer(d)}, device_id_type=MESH,
         )
         for n, d in enumerate(OFFSETS[:2])
@@ -151,8 +151,8 @@
     for copy in coup_copies:
         copy.start()
 
-    idx_row = idx_ref[...]
-    atom_row = atom_ref[...]
+    idx_row = idxv[...]
+    atom_row = atomv[...]
     atom_row = ((lax.shift_right_logical(atom_row, 5) - g + 33) & 31) * 32 + (atom_row & 31)
 
     def column(row):
@@ -170,10 +170,8 @@
     up_row = lax.broadcasted_iota(jnp.int32, (128, 2048), 0)
     up_lane = lax.broadcasted_iota(jnp.int32, (128, 2048), 1)
     exp_up[...] = jnp.where(lax.shift_right_logical(up_lane, 7) == up_row, 1.0, 0.0).astype(BF16)
-    for copy in loads:
-        copy.wait()
     projt[...] = jnp.swapaxes(projv[...].astype(F32), 0, 1)
-    pt = jnp.swapaxes(potv[...].astype(F32), 0, 1)
+    pt = potv[...].astype(F32)
     for j in range(3):
         e, o = pt[2 * j], pt[2 * j + 1]
         potc[3 * j] = e[:, :128]
@@ -194,13 +192,14 @@
 
     lax.fori_loop(0, A, wait_first, 0)
 
+    planes = jnp.swapaxes(recv1[...].reshape(768, 256).astype(F32).reshape(96, 8, 256), 0, 1)
     for y in range(T):
-        xbuf[y] = dot(lxv[y * N : (y + 1) * N, :], recv1[...].reshape(768, 256)).astype(BF16)
+        xbuf[y] = dot(cxv[...], planes[y].astype(BF16)).astype(BF16)
     for j in range(3):
         for b in range(2):
             cut = slice(b * 128, (b + 1) * 128)
             eo = jnp.concatenate([xbuf[2 * j, :, cut], xbuf[2 * j + 1, :, cut]], axis=1)
-            real = dot(eo, wz_ref[...]).astype(BF16)
+            real = dot(eo, wzv[...]).astype(BF16)
             for t in range(3):
                 rs[3 * j + t, :, cut] = real[:, t * 128 : (t + 1) * 128]
 
@@ -231,7 +230,7 @@
         copy.start()
     for copy in coup_copies:
         copy.wait()
-    coup = coup_in[0] + pltpu.roll(coup_ref[...], 32, 1) + pltpu.roll(coup_in[1], 64, 1)
+    coup = coup_in[0] + pltpu.roll(coup_out[...], 32, 1) + pltpu.roll(coup_in[1], 64, 1)
     for copy in coef_copies:
         copy.wait()
     lane16 = lax.broadcasted_iota(jnp.int32, (16, 128), 1)
@@ -272,14 +271,12 @@
         for b in range(2):
             cut = slice(b * 128, (b + 1) * 128)
             row = jnp.concatenate([mx[3 * j + t, :, cut] for t in range(3)], axis=1)
-            eo = dot(row, wzt_ref[...]).astype(BF16)
+            eo = dot(row, wztv[...]).astype(BF16)
             xbuf[2 * j, :, cut] = eo[:, :128]
             xbuf[2 * j + 1, :, cut] = eo[:, 128:]
-    xall = xbuf[...].reshape(T * N, 256)
-    for n in range(4):
-        send2[4 * n : 4 * n + 4] = (
-            dot(lxtv[n * N : (n + 1) * N, :], xall).astype(BF16).reshape(4, 3, 16, 256)
-        )
+    planes = [dot(cxtv[...], xbuf[y])[None] for y in range(T)] + [jnp.zeros((2, 96, 256), F32)]
+    planes = jnp.swapaxes(jnp.concatenate(planes, axis=0), 0, 1)
+    send2[...] = planes.reshape(768, 256).astype(BF16).reshape(A, 3, 16, 256)
 
     def second_copy(i):
         to = jnp.where(i < 8, i, i + 16)
@@ -365,26 +362,29 @@
 
 
 def shards(waves, potential, block_index, atom_of_slot, projectors, coupling):
-    cy, cyi, lx, lxt, wz, wzt = (jnp.asarray(x) for x in tables())
+    cy, cyi, cx, cxt, wz, wzt = (jnp.asarray(x) for x in tables())
     coup = jnp.transpose(coupling, (1, 2, 0)).reshape(64, 32)
-    coup = jnp.pad(coup, ((0, 0), (0, 96)))
-    any_spec = pl.BlockSpec(memory_space=pl.ANY)
-    vmem = pl.BlockSpec(memory_space=pltpu.VMEM)
+    hbm = pl.BlockSpec(memory_space=pltpu.HBM)
     dma = pltpu.SemaphoreType.DMA
     recv = pl.pallas_call(
         main_kernel,
         name="exchange_and_apply",
         out_shape=jax.ShapeDtypeStruct((G, 3, 16, 256), BF16),
-        in_specs=[any_spec, any_spec, vmem, vmem, any_spec, vmem, any_spec, any_spec, any_spec, vmem, vmem],
-        out_specs=any_spec,
+        in_specs=[hbm] * 11,
+        out_specs=hbm,
         scratch_shapes=[
             pltpu.VMEM((2, T, 48, N), BF16),
             pltpu.VMEM((2, T, 48, N), BF16),
             pltpu.VMEM((512, 192), BF16),
-            pltpu.VMEM((T * N, 768), BF16),
-            pltpu.VMEM((768, T * N), BF16),
-            pltpu.VMEM((N, T, N), BF16),
+            pltpu.VMEM((N, 96), BF16),
+            pltpu.VMEM((96, N), BF16),
+            pltpu.VMEM((256, 384), BF16),
+            pltpu.VMEM((384, 256), BF16),
+            pltpu.VMEM((T, N, N), BF16),
+            pltpu.VMEM((1, 512), jnp.int32),
+            pltpu.VMEM((1, 512), jnp.int32),
             pltpu.VMEM((512, 8, 128), BF16),
+            pltpu.VMEM((64, 32), F32),
             pltpu.VMEM((8, 512, 128), F32),
             pltpu.VMEM((9, N, 128), F32),
             pltpu.VMEM((9, 512, N), BF16),
@@ -397,10 +397,11 @@
             pltpu.VMEM((9, N, 256), BF16),
             pltpu.VMEM((9, N, 256), BF16),
             pltpu.VMEM((A, 3, 16, 256), BF16),
+            pltpu.VMEM((64, 128), F32),
+            pltpu.VMEM((2, 64, 128), F32),
             pltpu.VMEM((16, 128), F32),
             pltpu.VMEM((4, 16, 128), F32),
-            pltpu.VMEM((2, 64, 128), F32),
-            dma((7,)),
+            dma((12,)),
             dma((G,)),
             dma((A,)),
             dma((A,)),
@@ -412,11 +413,11 @@
             dma((2,)),
         ],
         compiler_params=pltpu.CompilerParams(
-            collective_id=0, has_side_effects=True, vmem_limit_bytes=48 << 20
+            collective_id=0, has_side_effects=True, vmem_limit_bytes=60 << 20
         ),
     )(
-        waves, potential, block_index.reshape(1, -1), atom_of_slot.reshape(1, -1), projectors, coup,
-        cy, lx, lxt, wz, wzt,
+        waves, jnp.transpose(potential, (1, 0, 2)), block_index.reshape(1, -1), atom_of_slot.reshape(1, -1),
+        projectors, coup, cy, cx, cxt, wz, wzt,
     )
     return pl.pallas_call(
         last_kernel,
@@ -429,7 +430,7 @@
             pl.BlockSpec((2, 2, N, N), lambda k: (0, k, 0, 0)),
         ],
         out_specs=pl.BlockSpec((2, 2, N, N), lambda k: (0, k, 0, 0)),
-        compiler_params=pltpu.CompilerParams(vmem_limit_bytes=32 << 20),
+        compiler_params=pltpu.CompilerParams(vmem_limit_bytes=60 << 20),
     )(cyi, recv, waves)
 
 

time: 64.1 us -> 57.2 us (0.89)
  local copies, waits for them, and re-layouts: 7.65 us -> 0 us
  Pallas kernels: 56.1 us -> 57 us
    unnamed x17 -> x0, local copies, waits for them, and re-layouts: 6.79 us -> none
    pallas_call x1, Pallas kernels: 2.21 us -> 3.75 us  [shards(): pl.pallas_call(last_kernel, name='finish', grid=(3,), out_shape=jax.Shape...]
    pad x1 -> x0, local copies, waits for them, and re-layouts: 0.86 us -> none  [shards(): coup = jnp.pad(coup, ((0, 0), (0, 96)))]
where the time goes in v2:
time: 57.2 us; the launch traced here: 57 us
  Pallas kernels  57 us (100%)
    pallas_call x1, Pallas kernels, shards(): pl.pallas_call(main_kernel, name='exchange_and_apply', out_shape=jax.Shap...  53.3 us
    pallas_call x1, Pallas kernels, shards(): pl.pallas_call(last_kernel, name='finish', grid=(3,), out_shape=jax.Shape...  3.75 us

profile of v2, /device:TPU:1, one launch (start us, length us, event | category | flops | bytes accessed | tf_op | source)
XLA Modules:
  0.0 57.0 jit_solution(12961880361529288018)
XLA Ops:
  0.0 53.3 %exchange_and_apply.1.recv = bf16[32,3,16,256]{3,2,1,0:T(8,128)(2,1)} custom-call(bf16[2,6,192,192]{3,2,1,0:T(8,128)(2,1)} %waves.3, bf16[6,192,192]{2,1,0:T(8,128)(2,1)} %bitcast.6, s32[1,512]{1,0:T(1,128)} %bitcast.8, s32[1,512]{1,0:T(1,128)} %bitcast.9, bf16[512,8,128]{2,1,0:T(8,128)(2,1)} %proj.1, f32[64,32]{1,0:T(8,128)} %bitcast.7, ...), custom_call_target="tpu_custom_call" | custom-call | tf_op jit(solution)/shard_map/exchange_and_apply/pallas_call | solution.py:369
  53.3 3.8 %finish.1 = bf16[2,6,192,192]{3,2,1,0:T(8,128)(2,1)} custom-call(bf16[192,512]{1,0:T(8,128)(2,1)} %constant.13.clone.cyi, bf16[32,3,16,256]{3,2,1,0:T(8,128)(2,1)} %exchange_and_apply.1.recv, bf16[2,6,192,192]{3,2,1,0:T(8,128)(2,1)} %waves.3), custom_call_target="tpu_custom_call" | custom-call | tf_op jit(solution)/shard_map/finish/pallas_call | solution.py:422

commit v3 on v2

--- a/solution.py
+++ b/solution.py
@@ -24,18 +24,15 @@
     angles = np.float32(2.0 * math.pi / N) * ((k[:, None] * k[None, :]) % N).astype(np.float32)
     c = ((np.cos(angles) + np.sin(angles)) / np.float32(math.sqrt(N))).astype(ml_dtypes.bfloat16)
     c = c.astype(np.float32)
-    cy = np.zeros((G, 2, 8, 2, 96), np.float32)
+    cy = np.zeros((G, 8, 96), np.float32)
+    cy[:, :T] = c[:, KEEP].reshape(G, T, 96)
+    cy = cy.reshape(256, 96)
+    cx = c[:, KEEP].reshape(N, A, T).transpose(0, 2, 1).reshape(N, 96)
+    wz = np.zeros((2, 2, 96, 2, 2, N), np.float32)
     for par in range(2):
-        cy[:, par, :T, par, :] = c[:, KEEP].reshape(G, T, 96)
-    cy = cy.reshape(512, 192)
-    cx = c[:, KEEP]
-    lane = np.arange(128)
-    kz = np.where(lane < 64, lane, lane + 64)
-    half = c[kz, :] * ((lane < 48) | (lane >= 80))[:, None]
-    wz = np.zeros((2, 128, 2, N), np.float32)
-    wz[0, :, 0, :] = half
-    wz[1, :, 1, :] = half
-    wz = wz.reshape(256, 384)
+        for b in range(2):
+            wz[par, b, :, b, par, :] = c[KEEP]
+    wz = wz.reshape(384, 768)
     out = [cy, cy.T, cx, cx.T, wz, wz.T]
     return [np.ascontiguousarray(x).astype(ml_dtypes.bfloat16) for x in out]
 
@@ -50,22 +47,27 @@
 
 
 def sphere_sq(kx):
-    row = lax.broadcasted_iota(jnp.int32, (96, 128), 0)
-    lane = lax.broadcasted_iota(jnp.int32, (96, 128), 1)
+    row = lax.broadcasted_iota(jnp.int32, (96, 96), 0)
+    lane = lax.broadcasted_iota(jnp.int32, (96, 96), 1)
     ky = jnp.where(row < 48, row, row + 96)
-    kz = jnp.where(lane < 64, lane, lane + 64)
+    kz = jnp.where(lane < 48, lane, lane + 96)
     return folded_sq(kx) + folded_sq(ky) + folded_sq(kz)
 
 
-def squeeze_z(w):
-    return jnp.concatenate([w[:, :64], w[:, 128:]], axis=1)
+def kept(low, high):
+    w = jnp.concatenate([low, high], axis=0).astype(F32)
+    return jnp.concatenate([w[:, :48], w[:, 144:]], axis=1)
+
+
+def tile(x, n):
+    return x[..., n * 128 : (n + 1) * 128]
 
 
 def main_kernel(
     waves, pot, idx, atom, proj, coup, cy, cx, cxt, wz, wzt, out,
     wlo, whi, cyv, cxv, cxtv, wzv, wztv, potv, idxv, atomv, projv, coupv,
     projt, potc, oh1, oh2, oha, exp_up,
-    send1, recv1, xbuf, rs, mx, send2, coup_out, coup_in, coef_out, coef_in,
+    send1, recv1, rs, mx, send2, coup_out, coup_in, coef_out, coef_in,
     load_sem, s1, r1, s2, r2, self_sem, cs, cr, ks, kr,
 ):
     g = lax.axis_index("grid")
@@ -106,19 +108,20 @@
     def _():
         for copy in wave_loads:
             copy.wait()
-        for kp in range(3):
-            parts = []
-            for par in range(2):
-                kx = g * T + 2 * kp + par
-                inside = sphere_sq(kx) < RAD2
-                cols = []
-                for b in range(2):
-                    w = jnp.concatenate([wlo[b, 2 * kp + par], whi[b, 2 * kp + par]], axis=0)
-                    w = squeeze_z(w.astype(F32))
-                    cols.append(jnp.where(inside, w, 0.0).astype(BF16))
-                parts.append(jnp.concatenate(cols, axis=1))
-            rhs = jnp.concatenate(parts, axis=0)
-            send1[:, kp] = dot(cyv[...], rhs).astype(BF16).reshape(G, 16, 256)
+        parts = []
+        for k in range(T):
+            inside = sphere_sq(g * T + k) < RAD2
+            for b in range(2):
+                parts.append(jnp.where(inside, kept(wlo[b, k], whi[b, k]), 0.0))
+        rhs = jnp.concatenate(parts, axis=1).astype(BF16)
+        spare = [dot(cyv[...], tile(rhs, n)).reshape(G, 8, 128) for n in (7, 8)]
+        sub = lax.broadcasted_iota(jnp.int32, (G, 8, 128), 1)
+        for t in range(7):
+            plane = dot(cyv[...], tile(rhs, t)).reshape(G, 8, 128)
+            if t < T:
+                plane = jnp.where(sub == 6, spare[0][:, t : t + 1, :], plane)
+                plane = jnp.where(sub == 7, spare[1][:, t : t + 1, :], plane)
+            send1[:, :, t * 128 : (t + 1) * 128] = plane.astype(BF16)
 
     pl.semaphore_wait(barrier, G - 1)
 
@@ -192,16 +195,17 @@
 
     lax.fori_loop(0, A, wait_first, 0)
 
-    planes = jnp.swapaxes(recv1[...].reshape(768, 256).astype(F32).reshape(96, 8, 256), 0, 1)
+    got = jnp.swapaxes(recv1[...].astype(F32), 0, 1)
+    stacks = []
     for y in range(T):
-        xbuf[y] = dot(cxv[...], planes[y].astype(BF16)).astype(BF16)
+        line = jnp.concatenate([got[y], tile(got[6], y), tile(got[7], y)], axis=1)
+        stacks.append(jnp.concatenate([line[:, k * N : (k + 1) * N] for k in range(T)], axis=0))
     for j in range(3):
-        for b in range(2):
-            cut = slice(b * 128, (b + 1) * 128)
-            eo = jnp.concatenate([xbuf[2 * j, :, cut], xbuf[2 * j + 1, :, cut]], axis=1)
-            real = dot(eo, wzv[...]).astype(BF16)
-            for t in range(3):
-                rs[3 * j + t, :, cut] = real[:, t * 128 : (t + 1) * 128]
+        rhs = jnp.concatenate([stacks[2 * j], stacks[2 * j + 1]], axis=1).astype(BF16)
+        part = dot(cxv[...], rhs).astype(BF16)
+        real = dot(part, wzv[...]).astype(BF16)
+        for t in range(3):
+            rs[3 * j + t] = jnp.concatenate([tile(real, t), tile(real, 3 + t)], axis=1)
 
     rows = dot(oh1[0], rs[0])
     for c in range(1, 9):
@@ -267,16 +271,23 @@
         local = potc[c]
         local = jnp.concatenate([local, local], axis=1)
         mx[c] = (local * rs[c].astype(F32) + spread).astype(BF16)
+    lines = []
     for j in range(3):
-        for b in range(2):
-            cut = slice(b * 128, (b + 1) * 128)
-            row = jnp.concatenate([mx[3 * j + t, :, cut] for t in range(3)], axis=1)
-            eo = dot(row, wztv[...]).astype(BF16)
-            xbuf[2 * j, :, cut] = eo[:, :128]
-            xbuf[2 * j + 1, :, cut] = eo[:, 128:]
-    planes = [dot(cxtv[...], xbuf[y])[None] for y in range(T)] + [jnp.zeros((2, 96, 256), F32)]
-    planes = jnp.swapaxes(jnp.concatenate(planes, axis=0), 0, 1)
-    send2[...] = planes.reshape(768, 256).astype(BF16).reshape(A, 3, 16, 256)
+        row = jnp.concatenate([tile(mx[3 * j + t], b) for b in range(2) for t in range(3)], axis=1)
+        part = dot(row, wztv[...]).astype(BF16)
+        back = dot(cxtv[...], part)
+        for par in range(2):
+            lines.append(
+                jnp.concatenate(
+                    [back[k * A : (k + 1) * A, par * N : (par + 1) * N] for k in range(T)], axis=1
+                )
+            )
+    spare = [
+        jnp.concatenate([tile(line, n) for line in lines] + [jnp.zeros((A, 128), F32)], axis=1)
+        for n in (7, 8)
+    ]
+    lines = jnp.concatenate([line[None, :, :896] for line in lines] + [x[None] for x in spare], axis=0)
+    send2[...] = jnp.swapaxes(lines, 0, 1).astype(BF16)
 
     def second_copy(i):
         to = jnp.where(i < 8, i, i + 16)
@@ -333,28 +344,35 @@
     lax.fori_loop(0, A, wait_back, 0)
 
 
-def last_kernel(cyi, recv, waves, out):
-    kp = pl.program_id(0)
+def last_kernel(cyt, recv, waves, out):
     g = lax.axis_index("grid")
     active = jnp.logical_or(g < 8, g >= 24)
 
     @pl.when(active)
     def _():
-        f = dot(cyi[...], recv[...].reshape(512, 256))
-        for par in range(2):
-            ksq = sphere_sq(g * T + 2 * kp + par)
+        got = recv[...].astype(F32)
+        sub = lax.broadcasted_iota(jnp.int32, (G, 8, 128), 1)
+        planes = [got]
+        for row in (6, 7):
+            spare = jnp.zeros((G, 8, 128), F32)
+            for y in range(T):
+                spare = jnp.where(sub == y, tile(got, y)[:, row : row + 1, :], spare)
+            planes.append(spare)
+        planes = jnp.concatenate(planes, axis=2).reshape(256, 1152).astype(BF16)
+        fifth = dot(cyt[...], planes)
+        for k in range(T):
+            ksq = sphere_sq(g * T + k)
             inside = ksq < RAD2
             kinetic = ksq.astype(F32) / RAD2
             for b in range(2):
-                w = jnp.concatenate([waves[b, par, 0:48, :], waves[b, par, 144:192, :]], axis=0)
-                w = squeeze_z(w.astype(F32))
-                part = f[par * 96 : (par + 1) * 96, b * 128 : (b + 1) * 128]
-                total = jnp.where(inside, kinetic * w + part, 0.0)
-                wide = jnp.concatenate([total[:, :64], jnp.zeros((96, 64), F32), total[:, 64:]], axis=1)
+                n = (2 * k + b) * 96
+                w = kept(waves[b, k, 0:48, :], waves[b, k, 144:192, :])
+                total = jnp.where(inside, kinetic * w + fifth[:, n : n + 96], 0.0)
+                wide = jnp.concatenate([total[:, :48], jnp.zeros((96, 96), F32), total[:, 48:]], axis=1)
                 wide = wide.astype(BF16)
-                out[b, par, 0:48, :] = wide[:48]
-                out[b, par, 48:144, :] = jnp.zeros((96, N), BF16)
-                out[b, par, 144:192, :] = wide[48:]
+                out[b, k, 0:48, :] = wide[:48]
+                out[b, k, 48:144, :] = jnp.zeros((96, N), BF16)
+                out[b, k, 144:192, :] = wide[48:]
 
     @pl.when(jnp.logical_not(active))
     def _():
@@ -362,24 +380,25 @@
 
 
 def shards(waves, potential, block_index, atom_of_slot, projectors, coupling):
-    cy, cyi, cx, cxt, wz, wzt = (jnp.asarray(x) for x in tables())
+    cy, cyt, cx, cxt, wz, wzt = (jnp.asarray(x) for x in tables())
     coup = jnp.transpose(coupling, (1, 2, 0)).reshape(64, 32)
     hbm = pl.BlockSpec(memory_space=pltpu.HBM)
+    vmem = pl.BlockSpec(memory_space=pltpu.VMEM)
     dma = pltpu.SemaphoreType.DMA
     recv = pl.pallas_call(
         main_kernel,
         name="exchange_and_apply",
-        out_shape=jax.ShapeDtypeStruct((G, 3, 16, 256), BF16),
+        out_shape=jax.ShapeDtypeStruct((G, 8, 896), BF16),
         in_specs=[hbm] * 11,
         out_specs=hbm,
         scratch_shapes=[
             pltpu.VMEM((2, T, 48, N), BF16),
             pltpu.VMEM((2, T, 48, N), BF16),
-            pltpu.VMEM((512, 192), BF16),
+            pltpu.VMEM((256, 96), BF16),
             pltpu.VMEM((N, 96), BF16),
             pltpu.VMEM((96, N), BF16),
-            pltpu.VMEM((256, 384), BF16),
-            pltpu.VMEM((384, 256), BF16),
+            pltpu.VMEM((384, 768), BF16),
+            pltpu.VMEM((768, 384), BF16),
             pltpu.VMEM((T, N, N), BF16),
             pltpu.VMEM((1, 512), jnp.int32),
             pltpu.VMEM((1, 512), jnp.int32),
@@ -391,12 +410,11 @@
             pltpu.VMEM((9, N, 512), BF16),
             pltpu.VMEM((512, 128), BF16),
             pltpu.VMEM((128, 2048), BF16),
-            pltpu.VMEM((G, 3, 16, 256), BF16),
-            pltpu.VMEM((A, 3, 16, 256), BF16),
-            pltpu.VMEM((T, N, 256), BF16),
+            pltpu.VMEM((G, 8, 896), BF16),
+            pltpu.VMEM((A, 8, 896), BF16),
             pltpu.VMEM((9, N, 256), BF16),
             pltpu.VMEM((9, N, 256), BF16),
-            pltpu.VMEM((A, 3, 16, 256), BF16),
+            pltpu.VMEM((A, 8, 896), BF16),
             pltpu.VMEM((64, 128), F32),
             pltpu.VMEM((2, 64, 128), F32),
             pltpu.VMEM((16, 128), F32),
@@ -422,16 +440,11 @@
     return pl.pallas_call(
         last_kernel,
         name="finish",
-        grid=(3,),
         out_shape=jax.ShapeDtypeStruct(waves.shape, BF16),
-        in_specs=[
-            pl.BlockSpec((192, 512), lambda k: (0, 0)),
-            pl.BlockSpec((G, 1, 16, 256), lambda k: (0, k, 0, 0)),
-            pl.BlockSpec((2, 2, N, N), lambda k: (0, k, 0, 0)),
-        ],
-        out_specs=pl.BlockSpec((2, 2, N, N), lambda k: (0, k, 0, 0)),
+        in_specs=[vmem] * 3,
+        out_specs=vmem,
         compiler_params=pltpu.CompilerParams(vmem_limit_bytes=60 << 20),
-    )(cyi, recv, waves)
+    )(cyt, recv, waves)
 
 
 def solution(mesh):

time: 57.2 us -> 46.5 us (0.81)
  Pallas kernels: 57 us -> 46.4 us
    pallas_call x1, Pallas kernels: 53.3 us -> 43.2 us  [shards(): pl.pallas_call(main_kernel, name='exchange_and_apply', out_shape=jax.Shap...]
    pallas_call x1, Pallas kernels: 3.75 us -> 3.17 us  [shards(): pl.pallas_call(last_kernel, name='finish', out_shape=jax.ShapeDtypeStruct...]
where the time goes in v3:
time: 46.5 us; the launch traced here: 46.4 us
  Pallas kernels  46.4 us (100%)
    pallas_call x1, Pallas kernels, shards(): pl.pallas_call(main_kernel, name='exchange_and_apply', out_shape=jax.Shap...  43.2 us
    pallas_call x1, Pallas kernels, shards(): pl.pallas_call(last_kernel, name='finish', out_shape=jax.ShapeDtypeStruct...  3.17 us

profile of v3, /device:TPU:1, one launch (start us, length us, event | category | flops | bytes accessed | tf_op | source)
XLA Modules:
  0.0 46.4 jit_solution(7367432748564201664)
XLA Ops:
  0.0 43.2 %exchange_and_apply.1.recv = bf16[32,8,896]{2,1,0:T(8,128)(2,1)} custom-call(bf16[2,6,192,192]{3,2,1,0:T(8,128)(2,1)} %waves.3, bf16[6,192,192]{2,1,0:T(8,128)(2,1)} %bitcast.6, s32[1,512]{1,0:T(1,128)} %bitcast.8, s32[1,512]{1,0:T(1,128)} %bitcast.9, bf16[512,8,128]{2,1,0:T(8,128)(2,1)} %proj.1, f32[64,32]{1,0:T(8,128)} %bitcast.7, ...), custom_call_target="tpu_custom_call" | custom-call | tf_op jit(solution)/shard_map/exchange_and_apply/pallas_call | solution.py:388
  43.2 3.2 %finish.1 = bf16[2,6,192,192]{3,2,1,0:T(8,128)(2,1)} custom-call(bf16[96,256]{1,0:T(8,128)(2,1)} %constant.13.clone.cyt, bf16[32,8,896]{2,1,0:T(8,128)(2,1)} %exchange_and_apply.1.recv, bf16[2,6,192,192]{3,2,1,0:T(8,128)(2,1)} %waves.3), custom_call_target="tpu_custom_call" | custom-call | tf_op jit(solution)/shard_map/finish/pallas_call | solution.py:440

commit v4 on v3

v4 whole, which is shorter than its diff:
```python
import functools
import math

import jax
import jax.numpy as jnp
import ml_dtypes
import numpy as np
from jax import lax
from jax.experimental import pallas as pl
from jax.experimental.pallas import tpu as pltpu
from jax.sharding import PartitionSpec as P

MESH = pl.DeviceIdType.MESH
F32, BF16 = jnp.float32, jnp.bfloat16
N, G, T = 192, 32, 6
A = 16
RAD2 = 48 * 48
KEEP = np.concatenate([np.arange(48), np.arange(144, 192)])
OFFSETS = (1, -1, 2, -2)
FIRST = ((0, 4, 0), (4, 3, 5))
SECOND = ((0, 3, 0), (3, 4, 4))


def tables():
    k = np.arange(N)
    angles = np.float32(2.0 * math.pi / N) * ((k[:, None] * k[None, :]) % N).astype(np.float32)
    c = ((np.cos(angles) + np.sin(angles)) / np.float32(math.sqrt(N))).astype(ml_dtypes.bfloat16)
    c = c.astype(np.float32)
    cy = np.zeros((G, 8, 96), np.float32)
    cy[:, :T] = c[:, KEEP].reshape(G, T, 96)
    cy = cy.reshape(256, 96)
    cx = c[:, KEEP].reshape(N, A, T).transpose(0, 2, 1).reshape(N, 96)
    wz = np.zeros((2, 96, 2, N), np.float32)
    for par in range(2):
        wz[par, :, par, :] = c[KEEP]
    wz = wz.reshape(192, 384)
    out = [cy, cy.T, cx, cx.T, wz, wz.T]
    return [np.ascontiguousarray(x).astype(ml_dtypes.bfloat16) for x in out]


def dot(a, b):
    return jnp.dot(a, b, preferred_element_type=F32)


def folded_sq(k):
    f = jnp.minimum(k, N - k)
    return f * f


def sphere_sq(kx):
    row = lax.broadcasted_iota(jnp.int32, (96, 96), 0)
    lane = lax.broadcasted_iota(jnp.int32, (96, 96), 1)
    ky = jnp.where(row < 48, row, row + 96)
    kz = jnp.where(lane < 48, lane, lane + 96)
    return folded_sq(kx) + folded_sq(ky) + folded_sq(kz)


def kept(low, high):
    w = jnp.concatenate([low, high], axis=0).astype(F32)
    return jnp.concatenate([w[:, :48], w[:, 144:]], axis=1)


def tile(x, n):
    return x[..., n * 128 : (n + 1) * 128]


def main_kernel(
    waves, pot, idx, atom, proj, coup, cy, cx, cxt, wz, wzt, out,
    wlo, whi, cyv, cxv, cxtv, wzv, wztv, potv, idxv, atomv, projv, coupv,
    projt, potc, oh1, oh2, oha, exp_up,
    send1, recv1, rs, send2, coup_out, coup_in, coef_out, coef_in,
    load_sem, s1, r1, s2, r2, self_sem, cs, cr, ks, kr,
):
    g = lax.axis_index("grid")
    active = jnp.logical_or(g < 8, g >= 24)
    ai = jnp.where(g < 8, g, g - 16)

    def peer(d):
        return lax.rem(g + d + G, G)

    wave_loads = [
        pltpu.make_async_copy(waves.at[:, :, 0:48, :], wlo, load_sem.at[0]),
        pltpu.make_async_copy(waves.at[:, :, 144:192, :], whi, load_sem.at[1]),
        pltpu.make_async_copy(cy, cyv, load_sem.at[2]),
    ]
    pairs = (
        (coup, coupv), (idx, idxv), (atom, atomv), (proj, projv), (pot, potv),
        (cx, cxv), (wz, wzv), (wzt, wztv), (cxt, cxtv),
    )
    loads = [pltpu.make_async_copy(a, b, load_sem.at[3 + n]) for n, (a, b) in enumerate(pairs)]

    @pl.when(active)
    def _():
        for copy in wave_loads:
            copy.start()

    for copy in loads:
        copy.start()

    barrier = pltpu.get_barrier_semaphore()

    def greet(d, carry):
        pl.semaphore_signal(barrier, inc=1, device_id={"grid": peer(d)}, device_id_type=MESH)
        return carry

    lax.fori_loop(1, G, greet, 0)

    @pl.when(active)
    def _():
        for copy in wave_loads:
            copy.wait()
        parts = []
        for b in range(2):
            for k in range(T):
                inside = sphere_sq(g * T + k) < RAD2
                parts.append(jnp.where(inside, kept(wlo[b, k], whi[b, k]), 0.0))
        rhs = jnp.concatenate(parts, axis=1).astype(BF16)
        sub = lax.broadcasted_iota(jnp.int32, (G, 8, 128), 1)
        for wire, count, begin in FIRST:
            spare = dot(cyv[...], tile(rhs, begin + count)).reshape(G, 8, 128)
            for t in range(count):
                plane = dot(cyv[...], tile(rhs, begin + t)).reshape(G, 8, 128)
                for row, y in ((6, t), (7, t + count)):
                    if y < T:
                        plane = jnp.where(sub == row, spare[:, y : y + 1, :], plane)
                send1[:, :, (wire + t) * 128 : (wire + t + 1) * 128] = plane.astype(BF16)

    pl.semaphore_wait(barrier, G - 1)

    def half(ref, i, plan, h):
        return ref.at[i, :, pl.ds(plan[h][0] * 128, plan[h][1] * 128)]

    def first_copy(d, h):
        to = peer(d)
        return pltpu.make_async_remote_copy(
            src_ref=half(send1, to, FIRST, h), dst_ref=half(recv1, ai, FIRST, h),
            send_sem=s1.at[h, d], recv_sem=r1.at[h, ai],
            device_id={"grid": to}, device_id_type=MESH,
        )

    @pl.when(active)
    def _():
        for h in range(2):

            def go(d, carry):
                first_copy(d, h).start()
                return carry

            lax.fori_loop(1, G, go, 0)
        recv1[ai] = send1[g]

    for copy in loads:
        copy.wait()
    coup_out[...] = jnp.concatenate([coupv[...], jnp.zeros((64, 96), F32)], axis=1)
    coup_copies = [
        pltpu.make_async_remote_copy(
            src_ref=coup_out, dst_ref=coup_in.at[n], send_sem=ks.at[n], recv_sem=kr.at[n],
            device_id={"grid": peer(d)}, device_id_type=MESH,
        )
        for n, d in enumerate(OFFSETS[:2])
    ]
    for copy in coup_copies:
        copy.start()

    idx_row = idxv[...]
    atom_row = atomv[...]
    atom_row = ((lax.shift_right_logical(atom_row, 5) - g + 33) & 31) * 32 + (atom_row & 31)

    def column(row):
        return jnp.transpose(jnp.broadcast_to(row.astype(F32), (128, 512))).astype(jnp.int32)

    idx_col = column(idx_row)
    idx_col = jnp.concatenate([idx_col, idx_col[:, :64]], axis=1)
    lane192 = lax.broadcasted_iota(jnp.int32, (512, N), 1) * 9
    row192 = lax.broadcasted_iota(jnp.int32, (N, 512), 0) * 9
    for c in range(9):
        oh1[c] = jnp.where(lane192 + c == idx_col, 1.0, 0.0).astype(BF16)
        oh2[c] = jnp.where(row192 + c == idx_row, 1.0, 0.0).astype(BF16)
    lane128 = lax.broadcasted_iota(jnp.int32, (512, 128), 1)
    oha[...] = jnp.where(column(atom_row) == lane128, 1.0, 0.0).astype(BF16)
    up_row = lax.broadcasted_iota(jnp.int32, (128, 1024), 0)
    up_lane = lax.broadcasted_iota(jnp.int32, (128, 1024), 1)
    exp_up[...] = jnp.where(lax.shift_right_logical(up_lane, 7) == up_row, 1.0, 0.0).astype(BF16)
    projt[...] = jnp.swapaxes(projv[...].astype(F32), 0, 1)
    pt = potv[...].astype(F32)
    for j in range(3):
        e, o = pt[2 * j], pt[2 * j + 1]
        potc[3 * j] = e[:, :128]
        potc[3 * j + 1] = jnp.concatenate([e[:, 128:], o[:, :64]], axis=1)
        potc[3 * j + 2] = o[:, 64:]

    def wait_first(h):
        def body(i, carry):
            src = jnp.where(i < 8, i, i + 16)

            @pl.when(src != g)
            def _():
                pltpu.make_async_remote_copy(
                    src_ref=half(send1, 0, FIRST, h), dst_ref=half(recv1, i, FIRST, h),
                    send_sem=s1.at[h, 0], recv_sem=r1.at[h, i],
                    device_id={"grid": src}, device_id_type=MESH,
                ).wait_recv()

            return carry

        lax.fori_loop(0, A, body, 0)

    def arrived(h):
        wire, count, _ = FIRST[h]
        return jnp.swapaxes(recv1[:, :, wire * 128 : (wire + count) * 128].astype(F32), 0, 1)

    def folded(got, y, count):
        return tile(got[6 + y // count], y % count)

    def coef_copies(b):
        return [
            pltpu.make_async_remote_copy(
                src_ref=coef_out.at[b], dst_ref=coef_in.at[b, n], send_sem=cs.at[b, n], recv_sem=cr.at[b, n],
                device_id={"grid": peer(d)}, device_id_type=MESH,
            )
            for n, d in enumerate(OFFSETS)
        ]

    def project(b, lines):
        stacks = [
            jnp.concatenate([line[:, k * 96 : (k + 1) * 96] for k in range(T)], axis=0) for line in lines
        ]
        for j in range(3):
            rhs = jnp.concatenate([stacks[2 * j], stacks[2 * j + 1]], axis=1).astype(BF16)
            part = dot(cxv[...], rhs).astype(BF16)
            real = dot(part, wzv[...]).astype(BF16)
            for t in range(3):
                rs[b, 3 * j + t] = tile(real, t)
        rows = dot(oh1[0], rs[b, 0])
        for c in range(1, 9):
            rows = rows + dot(oh1[c], rs[b, c])
        prod = jnp.concatenate([(projt[p] * rows).astype(BF16) for p in range(8)], axis=1)
        inter = lax.dot_general(
            prod, exp_up[...], (((1,), (1,)), ((), ())), preferred_element_type=F32
        )
        inter = jnp.transpose(inter)[:16]
        high = inter.astype(BF16)
        low = (inter - high.astype(F32)).astype(BF16)
        coef_out[b] = (dot(high, oha[...]) + dot(low, oha[...]))[:8]
        for copy in coef_copies(b):
            copy.start()

    def apply(b, coup):
        for copy in coef_copies(b):
            copy.wait()
        lane = lax.broadcasted_iota(jnp.int32, (8, 128), 1)
        coef = coef_out[b] + pltpu.roll(coef_in[b, 0], 96, 1) + pltpu.roll(coef_in[b, 1], 32, 1)
        coef = coef + jnp.where(lane < 32, pltpu.roll(coef_in[b, 2], 64, 1), 0.0)
        coef = coef + jnp.where(
            jnp.logical_and(lane >= 64, lane < 96), pltpu.roll(coef_in[b, 3], 64, 1), 0.0
        )
        coupled = [jnp.sum(coup[8 * p : 8 * p + 8] * coef, axis=0, keepdims=True) for p in range(8)]
        coupled = jnp.concatenate(coupled + [jnp.zeros((120, 128), F32)], axis=0).astype(BF16)
        chosen = lax.dot_general(
            oha[...], coupled, (((1,), (1,)), ((), ())), preferred_element_type=F32
        ).astype(BF16)
        back = projt[0] * dot(chosen, tile(exp_up[...], 0))
        for p in range(1, 8):
            back = back + projt[p] * dot(chosen, tile(exp_up[...], p))
        back = back.astype(BF16)
        lines = []
        for j in range(3):
            row = []
            for c in range(3 * j, 3 * j + 3):
                row.append((potc[c] * rs[b, c].astype(F32) + dot(oh2[c], back)).astype(BF16))
            part = dot(jnp.concatenate(row, axis=1), wztv[...]).astype(BF16)
            part = dot(cxtv[...], part)
            for par in range(2):
                lines.append(
                    jnp.concatenate(
                        [part[k * A : (k + 1) * A, par * 96 : (par + 1) * 96] for k in range(T)], axis=1
                    )
                )
        return lines

    def second_copy(i, h):
        to = jnp.where(i < 8, i, i + 16)
        return to, pltpu.make_async_remote_copy(
            src_ref=half(send2, i, SECOND, h), dst_ref=half(out, g, SECOND, h),
            send_sem=s2.at[h, i], recv_sem=r2.at[h, g],
            device_id={"grid": to}, device_id_type=MESH,
        )

    def send_back(lines, h):
        wire, count, _ = SECOND[h]
        rows = [line[:, : count * 128] for line in lines]
        for first in (0, count):
            spare = [
                lines[y][:, count * 128 :] if y < T else jnp.zeros((A, 128), F32)
                for y in range(first, first + count)
            ]
            rows.append(jnp.concatenate(spare, axis=1))
        rows = jnp.concatenate([row[None] for row in rows], axis=0)
        send2[:, :, wire * 128 : (wire + count) * 128] = jnp.swapaxes(rows, 0, 1).astype(BF16)

        def go(n, carry):
            i = lax.rem(n + g, A)
            to, copy = second_copy(i, h)

            @pl.when(to != g)
            def _():
                copy.start()

            return carry

        lax.fori_loop(0, A, go, 0)

    wait_first(0)
    got = arrived(0)
    tails = [folded(got, y, 4) for y in range(T)]
    project(0, [jnp.concatenate([got[y], tails[y][:, :64]], axis=1) for y in range(T)])
    wait_first(1)
    got = arrived(1)
    project(1, [jnp.concatenate([tails[y][:, 64:], got[y], folded(got, y, 3)], axis=1) for y in range(T)])
    for copy in coup_copies:
        copy.wait()
    coup = coup_in[0] + pltpu.roll(coup_out[...], 32, 1) + pltpu.roll(coup_in[1], 64, 1)
    lines0 = apply(0, coup)
    send_back([line[:, :512] for line in lines0], 0)
    lines1 = apply(1, coup)
    send_back([jnp.concatenate([a[:, 512:], b], axis=1) for a, b in zip(lines0, lines1)], 1)

    @pl.when(active)
    def _():
        own = pltpu.make_async_copy(send2.at[ai], out.at[g], self_sem)
        own.start()
        own.wait()
        for h in range(2):

            def wait_sent(d, carry):
                first_copy(d, h).wait_send()
                return carry

            lax.fori_loop(1, G, wait_sent, 0)

            def wait_second(src, carry):
                @pl.when(src != g)
                def _():
                    pltpu.make_async_remote_copy(
                        src_ref=half(send2, 0, SECOND, h), dst_ref=half(out, src, SECOND, h),
                        send_sem=s2.at[h, 0], recv_sem=r2.at[h, src],
                        device_id={"grid": src}, device_id_type=MESH,
                    ).wait_recv()

                return carry

            lax.fori_loop(0, G, wait_second, 0)

    for h in range(2):

        def wait_back(i, carry):
            to, copy = second_copy(i, h)

            @pl.when(to != g)
            def _():
                copy.wait_send()

            return carry

        lax.fori_loop(0, A, wait_back, 0)


def last_kernel(cyt, recv, waves, out):
    g = lax.axis_index("grid")
    active = jnp.logical_or(g < 8, g >= 24)

    @pl.when(active)
    def _():
        got = recv[...].astype(F32)
        sub = lax.broadcasted_iota(jnp.int32, (G, 8, 128), 1)
        planes = []
        for wire, count, _ in SECOND:
            planes += [tile(got, wire + t) for t in range(count)]
            spare = jnp.zeros((G, 8, 128), F32)
            for y in range(T):
                row = 6 + y // count
                spare = jnp.where(sub == y, tile(got, wire + y % count)[:, row : row + 1, :], spare)
            planes.append(spare)
        planes = jnp.concatenate(planes, axis=2).reshape(256, 1152).astype(BF16)
        fifth = dot(cyt[...], planes)
        for k in range(T):
            ksq = sphere_sq(g * T + k)
            inside = ksq < RAD2
            kinetic = ksq.astype(F32) / RAD2
            for b in range(2):
                n = (b * T + k) * 96
                w = kept(waves[b, k, 0:48, :], waves[b, k, 144:192, :])
                total = jnp.where(inside, kinetic * w + fifth[:, n : n + 96], 0.0)
                wide = jnp.concatenate([total[:, :48], jnp.zeros((96, 96), F32), total[:, 48:]], axis=1)
                wide = wide.astype(BF16)
                out[b, k, 0:48, :] = wide[:48]
                out[b, k, 48:144, :] = jnp.zeros((96, N), BF16)
                out[b, k, 144:192, :] = wide[48:]

    @pl.when(jnp.logical_not(active))
    def _():
        out[...] = jnp.zeros(out.shape, BF16)


def shards(waves, potential, block_index, atom_of_slot, projectors, coupling):
    cy, cyt, cx, cxt, wz, wzt = (jnp.asarray(x) for x in tables())
    coup = jnp.transpose(coupling, (1, 2, 0)).reshape(64, 32)
    hbm = pl.BlockSpec(memory_space=pltpu.HBM)
    vmem = pl.BlockSpec(memory_space=pltpu.VMEM)
    dma = pltpu.SemaphoreType.DMA
    recv = pl.pallas_call(
        main_kernel,
        name="exchange_and_apply",
        out_shape=jax.ShapeDtypeStruct((G, 8, 896), BF16),
        in_specs=[hbm] * 11,
        out_specs=hbm,
        scratch_shapes=[
            pltpu.VMEM((2, T, 48, N), BF16),
            pltpu.VMEM((2, T, 48, N), BF16),
            pltpu.VMEM((256, 96), BF16),
            pltpu.VMEM((N, 96), BF16),
            pltpu.VMEM((96, N), BF16),
            pltpu.VMEM((192, 384), BF16),
            pltpu.VMEM((384, 192), BF16),
            pltpu.VMEM((T, N, N), BF16),
            pltpu.VMEM((1, 512), jnp.int32),
            pltpu.VMEM((1, 512), jnp.int32),
            pltpu.VMEM((512, 8, 128), BF16),
            pltpu.VMEM((64, 32), F32),
            pltpu.VMEM((8, 512, 128), F32),
            pltpu.VMEM((9, N, 128), F32),
            pltpu.VMEM((9, 512, N), BF16),
            pltpu.VMEM((9, N, 512), BF16),
            pltpu.VMEM((512, 128), BF16),
            pltpu.VMEM((128, 1024), BF16),
            pltpu.VMEM((G, 8, 896), BF16),
            pltpu.VMEM((A, 8, 896), BF16),
            pltpu.VMEM((2, 9, N, 128), BF16),
            pltpu.VMEM((A, 8, 896), BF16),
            pltpu.VMEM((64, 128), F32),
            pltpu.VMEM((2, 64, 128), F32),
            pltpu.VMEM((2, 8, 128), F32),
            pltpu.VMEM((2, 4, 8, 128), F32),
            dma((12,)),
            dma((2, G)),
            dma((2, A)),
            dma((2, A)),
            dma((2, G)),
            dma,
            dma((2, 4)),
            dma((2, 4)),
            dma((2,)),
            dma((2,)),
        ],
        compiler_params=pltpu.CompilerParams(
            collective_id=0, has_side_effects=True, vmem_limit_bytes=60 << 20
        ),
    )(
        waves, jnp.transpose(potential, (1, 0, 2)), block_index.reshape(1, -1), atom_of_slot.reshape(1, -1),
        projectors, coup, cy, cx, cxt, wz, wzt,
    )
    return pl.pallas_call(
        last_kernel,
        name="finish",
        out_shape=jax.ShapeDtypeStruct(waves.shape, BF16),
        in_specs=[vmem] * 3,
        out_specs=vmem,
        compiler_params=pltpu.CompilerParams(vmem_limit_bytes=60 << 20),
    )(cyt, recv, waves)


def solution(mesh):
    in_specs = (
        P("band", "grid", None, None),
        P(None, "grid", None),
        P("grid"),
        P("grid"),
        P("grid", None, None),
        P("grid", None, None),
    )
    out_specs = P("band", "grid", None, None)
    return jax.shard_map(shards, mesh=mesh, in_specs=in_specs, out_specs=out_specs, check_vma=False)
```

time: 46.5 us -> 45.8 us (0.985)
  Pallas kernels: 46.4 us -> 45.7 us
    pallas_call x1, Pallas kernels: 43.2 us -> 42.5 us  [shards(): pl.pallas_call(main_kernel, name='exchange_and_apply', out_shape=jax.Shap...]
where the time goes in v4:
time: 45.8 us; the launch traced here: 45.7 us
  Pallas kernels  45.7 us (100%)
    pallas_call x1, Pallas kernels, shards(): pl.pallas_call(main_kernel, name='exchange_and_apply', out_shape=jax.Shap...  42.5 us
    pallas_call x1, Pallas kernels, shards(): pl.pallas_call(last_kernel, name='finish', out_shape=jax.ShapeDtypeStruct...  3.14 us

profile of v4, /device:TPU:1, one launch (start us, length us, event | category | flops | bytes accessed | tf_op | source)
XLA Modules:
  0.0 45.7 jit_solution(5987330364518877804)
XLA Ops:
  0.0 42.5 %exchange_and_apply.1.recv = bf16[32,8,896]{2,1,0:T(8,128)(2,1)} custom-call(bf16[2,6,192,192]{3,2,1,0:T(8,128)(2,1)} %waves.3, bf16[6,192,192]{2,1,0:T(8,128)(2,1)} %bitcast.6, s32[1,512]{1,0:T(1,128)} %bitcast.8, s32[1,512]{1,0:T(1,128)} %bitcast.9, bf16[512,8,128]{2,1,0:T(8,128)(2,1)} %proj.1, f32[64,32]{1,0:T(8,128)} %bitcast.7, ...), custom_call_target="tpu_custom_call" | custom-call | tf_op jit(solution)/shard_map/exchange_and_apply/pallas_call | solution.py:411
  42.5 3.1 %finish.1 = bf16[2,6,192,192]{3,2,1,0:T(8,128)(2,1)} custom-call(bf16[96,256]{1,0:T(8,128)(2,1)} %constant.13.clone.cyt, bf16[32,8,896]{2,1,0:T(8,128)(2,1)} %exchange_and_apply.1.recv, bf16[2,6,192,192]{3,2,1,0:T(8,128)(2,1)} %waves.3), custom_call_target="tpu_custom_call" | custom-call | tf_op jit(solution)/shard_map/finish/pallas_call | solution.py:462

commit v5 on v3

--- a/solution.py
+++ b/solution.py
@@ -17,6 +17,7 @@
 RAD2 = 48 * 48
 KEEP = np.concatenate([np.arange(48), np.arange(144, 192)])
 OFFSETS = (1, -1, 2, -2)
+DIRECT = 512
 
 
 def tables():
@@ -67,8 +68,8 @@
     waves, pot, idx, atom, proj, coup, cy, cx, cxt, wz, wzt, out,
     wlo, whi, cyv, cxv, cxtv, wzv, wztv, potv, idxv, atomv, projv, coupv,
     projt, potc, oh1, oh2, oha, exp_up,
-    send1, recv1, rs, mx, send2, coup_out, coup_in, coef_out, coef_in,
-    load_sem, s1, r1, s2, r2, self_sem, cs, cr, ks, kr,
+    send1, recv1, rel1, rs, mx, send2, rel2, coup_out, coup_in, coef_out, coef_in,
+    load_sem, s1, s1b, r1, r1b, rr1, f1, s2, s2b, r2, r2b, rr2, f2, self_sem, cs, cr, ks, kr,
 ):
     g = lax.axis_index("grid")
     active = jnp.logical_or(g < 8, g >= 24)
@@ -125,20 +126,61 @@
 
     pl.semaphore_wait(barrier, G - 1)
 
-    def first_copy(d):
-        to = peer(d)
+    my_row = g // A
+    partner = lax.rem(g + A, G)
+    head = (slice(None), pl.ds(0, DIRECT))
+    tail = (slice(None), pl.ds(DIRECT, 896 - DIRECT))
+
+    def remote(src, dst, send, recv, to):
         return pltpu.make_async_remote_copy(
-            src_ref=send1.at[to], dst_ref=recv1.at[ai], send_sem=s1.at[d], recv_sem=r1.at[ai],
+            src_ref=src, dst_ref=dst, send_sem=send, recv_sem=recv,
             device_id={"grid": to}, device_id_type=MESH,
         )
 
+    def owner(i):
+        return jnp.where(i < 8, i, i + 16)
+
+    def is_whole(a):
+        return jnp.logical_or(a // A == my_row, a == partner)
+
+    def each(low, high, start, skip, body):
+        def step(n, carry):
+            i = low + lax.rem(n + start, high - low)
+
+            @pl.when(jnp.logical_not(skip(i)))
+            def _():
+                body(i)
+
+            return carry
+
+        lax.fori_loop(0, high - low, step, 0)
+
+    def itself(a):
+        return a == g
+
+    def forwarded1(to):
+        return remote(
+            send1.at[(to, *tail)], rel1.at[lax.rem(ai, 8)], s1b.at[to], rr1.at[lax.rem(ai, 8)],
+            lax.rem(to + A, G),
+        )
+
+    def whole1(to):
+        return remote(send1.at[to], recv1.at[ai], s1.at[to], r1.at[ai], to)
+
+    def part1(to):
+        return remote(send1.at[(to, *head)], recv1.at[(ai, *head)], s1.at[to], r1.at[ai], to)
+
+    def either(test, yes, no):
+        pl.when(test)(yes)
+        pl.when(jnp.logical_not(test))(no)
+
     @pl.when(active)
     def _():
-        def go(d, carry):
-            first_copy(d).start()
-            return carry
-
-        lax.fori_loop(1, G, go, 0)
+        each(0, G, g, is_whole, lambda to: forwarded1(to).start())
+        each(
+            0, G, g, itself,
+            lambda to: either(is_whole(to), lambda: whole1(to).start(), lambda: part1(to).start()),
+        )
         recv1[ai] = send1[g]
 
     for copy in loads:
@@ -181,19 +223,33 @@
         potc[3 * j + 1] = jnp.concatenate([e[:, 128:], o[:, :64]], axis=1)
         potc[3 * j + 2] = o[:, 64:]
 
-    def wait_first(i, carry):
-        src = jnp.where(i < 8, i, i + 16)
-
-        @pl.when(src != g)
-        def _():
-            pltpu.make_async_remote_copy(
-                src_ref=send1.at[0], dst_ref=recv1.at[i], send_sem=s1.at[0], recv_sem=r1.at[i],
-                device_id={"grid": src}, device_id_type=MESH,
-            ).wait_recv()
-
-        return carry
-
-    lax.fori_loop(0, A, wait_first, 0)
+    def pass1(k):
+        i = my_row * 8 + k
+        return remote(rel1.at[k], recv1.at[(i, *tail)], f1.at[k], r1b.at[i], partner)
+
+    def relay1(k):
+        remote(send1.at[(0, *tail)], rel1.at[k], s1b.at[0], rr1.at[k], partner).wait_recv()
+        pass1(k).start()
+
+    def own_row(k):
+        return owner(my_row * 8 + k) == g
+
+    each(0, 8, 0, own_row, relay1)
+
+    def wait1(i):
+        src = owner(i)
+
+        def parts():
+            remote(send1.at[(0, *head)], recv1.at[(i, *head)], s1.at[0], r1.at[i], src).wait_recv()
+            remote(rel1.at[0], recv1.at[(i, *tail)], f1.at[0], r1b.at[i], partner).wait_recv()
+
+        either(
+            is_whole(src),
+            lambda: remote(send1.at[0], recv1.at[i], s1.at[0], r1.at[i], src).wait_recv(),
+            parts,
+        )
+
+    each(0, A, 0, lambda i: owner(i) == g, wait1)
 
     got = jnp.swapaxes(recv1[...].astype(F32), 0, 1)
     stacks = []
@@ -262,12 +318,10 @@
             term = projt[p] * dot(chosen, exp_up[:, n : n + 128])
             back = term if back is None else back + term
         backs.append(back)
-    back = jnp.concatenate(backs, axis=1)
-    high = back.astype(BF16)
-    low = (back - high.astype(F32)).astype(BF16)
+    back = jnp.concatenate(backs, axis=1).astype(BF16)
 
     for c in range(9):
-        spread = dot(oh2[c], high) + dot(oh2[c], low)
+        spread = dot(oh2[c], back)
         local = potc[c]
         local = jnp.concatenate([local, local], axis=1)
         mx[c] = (local * rs[c].astype(F32) + spread).astype(BF16)
@@ -289,59 +343,70 @@
     lines = jnp.concatenate([line[None, :, :896] for line in lines] + [x[None] for x in spare], axis=0)
     send2[...] = jnp.swapaxes(lines, 0, 1).astype(BF16)
 
-    def second_copy(i):
-        to = jnp.where(i < 8, i, i + 16)
-        return to, pltpu.make_async_remote_copy(
-            src_ref=send2.at[i], dst_ref=out.at[g], send_sem=s2.at[i], recv_sem=r2.at[g],
-            device_id={"grid": to}, device_id_type=MESH,
-        )
-
-    def go_back(n, carry):
-        i = lax.rem(n + g, A)
-        to, copy = second_copy(i)
-
-        @pl.when(to != g)
-        def _():
-            copy.start()
-
-        return carry
-
-    lax.fori_loop(0, A, go_back, 0)
+    slot = lax.rem(g, A)
+
+    def forwarded2(i):
+        return remote(
+            send2.at[(i, *tail)], rel2.at[slot], s2b.at[i], rr2.at[slot], lax.rem(owner(i) + A, G)
+        )
+
+    def whole2(i):
+        return remote(send2.at[i], out.at[g], s2.at[i], r2.at[g], owner(i))
+
+    def part2(i):
+        return remote(send2.at[(i, *head)], out.at[(g, *head)], s2.at[i], r2.at[g], owner(i))
+
+    each(0, A, slot, lambda i: is_whole(owner(i)), lambda i: forwarded2(i).start())
+    each(
+        0, A, slot, lambda i: owner(i) == g,
+        lambda i: either(is_whole(owner(i)), lambda: whole2(i).start(), lambda: part2(i).start()),
+    )
+
+    def pass2(k):
+        src = my_row * A + k
+        return remote(rel2.at[k], out.at[(src, *tail)], f2.at[k], r2b.at[src], partner)
+
+    def relay2(k):
+        remote(send2.at[(0, *tail)], rel2.at[k], s2b.at[0], rr2.at[k], partner).wait_recv()
+        pass2(k).start()
+
+    @pl.when(jnp.logical_not(active))
+    def _():
+        each(0, A, 0, lambda k: k == slot, relay2)
+        each(0, A, 0, lambda k: k == slot, lambda k: pass2(k).wait_send())
+
+    def wait2(src):
+        def parts():
+            remote(send2.at[(0, *head)], out.at[(src, *head)], s2.at[0], r2.at[src], src).wait_recv()
+            remote(rel2.at[0], out.at[(src, *tail)], f2.at[0], r2b.at[src], partner).wait_recv()
+
+        either(
+            is_whole(src),
+            lambda: remote(send2.at[0], out.at[src], s2.at[0], r2.at[src], src).wait_recv(),
+            parts,
+        )
+
+    each(0, 8, 0, own_row, lambda k: pass1(k).wait_send())
 
     @pl.when(active)
     def _():
         own = pltpu.make_async_copy(send2.at[ai], out.at[g], self_sem)
         own.start()
         own.wait()
-
-        def wait_sent(d, carry):
-            first_copy(d).wait_send()
-            return carry
-
-        lax.fori_loop(1, G, wait_sent, 0)
-
-        def wait_second(src, carry):
-            @pl.when(src != g)
-            def _():
-                pltpu.make_async_remote_copy(
-                    src_ref=send2.at[0], dst_ref=out.at[src], send_sem=s2.at[0], recv_sem=r2.at[src],
-                    device_id={"grid": src}, device_id_type=MESH,
-                ).wait_recv()
-
-            return carry
-
-        lax.fori_loop(0, G, wait_second, 0)
-
-    def wait_back(i, carry):
-        to, copy = second_copy(i)
-
-        @pl.when(to != g)
-        def _():
-            copy.wait_send()
-
-        return carry
-
-    lax.fori_loop(0, A, wait_back, 0)
+        each(0, G, 0, is_whole, lambda to: forwarded1(to).wait_send())
+        each(
+            0, G, 0, itself,
+            lambda to: either(is_whole(to), lambda: whole1(to).wait_send(), lambda: part1(to).wait_send()),
+        )
+        each(0, G, 0, itself, wait2)
+
+    each(0, A, 0, lambda i: is_whole(owner(i)), lambda i: forwarded2(i).wait_send())
+    each(
+        0, A, 0, lambda i: owner(i) == g,
+        lambda i: either(
+            is_whole(owner(i)), lambda: whole2(i).wait_send(), lambda: part2(i).wait_send()
+        ),
+    )
 
 
 def last_kernel(cyt, recv, waves, out):
@@ -412,18 +477,28 @@
             pltpu.VMEM((128, 2048), BF16),
             pltpu.VMEM((G, 8, 896), BF16),
             pltpu.VMEM((A, 8, 896), BF16),
+            pltpu.VMEM((8, 8, 896 - DIRECT), BF16),
             pltpu.VMEM((9, N, 256), BF16),
             pltpu.VMEM((9, N, 256), BF16),
             pltpu.VMEM((A, 8, 896), BF16),
+            pltpu.VMEM((A, 8, 896 - DIRECT), BF16),
             pltpu.VMEM((64, 128), F32),
             pltpu.VMEM((2, 64, 128), F32),
             pltpu.VMEM((16, 128), F32),
             pltpu.VMEM((4, 16, 128), F32),
             dma((12,)),
             dma((G,)),
+            dma((G,)),
+            dma((A,)),
+            dma((A,)),
+            dma((8,)),
+            dma((8,)),
             dma((A,)),
             dma((A,)),
             dma((G,)),
+            dma((G,)),
+            dma((A,)),
+            dma((A,)),
             dma,
             dma((4,)),
             dma((4,)),

time: 46.5 us -> 47.3 us (1.017)
  Pallas kernels: 46.4 us -> 47.1 us
    pallas_call x1, Pallas kernels: 43.2 us -> 44 us  [shards(): pl.pallas_call(main_kernel, name='exchange_and_apply', out_shape=jax.Shap...]
where the time goes in v5:
time: 47.3 us; the launch traced here: 47.1 us
  Pallas kernels  47.1 us (100%)
    pallas_call x1, Pallas kernels, shards(): pl.pallas_call(main_kernel, name='exchange_and_apply', out_shape=jax.Shap...  44 us
    pallas_call x1, Pallas kernels, shards(): pl.pallas_call(last_kernel, name='finish', out_shape=jax.ShapeDtypeStruct...  3.17 us

profile of v5, /device:TPU:1, one launch (start us, length us, event | category | flops | bytes accessed | tf_op | source)
XLA Modules:
  0.0 47.1 jit_solution(6624029640204974867)
XLA Ops:
  0.0 44.0 %exchange_and_apply.1.recv = bf16[32,8,896]{2,1,0:T(8,128)(2,1)} custom-call(bf16[2,6,192,192]{3,2,1,0:T(8,128)(2,1)} %waves.3, bf16[6,192,192]{2,1,0:T(8,128)(2,1)} %bitcast.6, s32[1,512]{1,0:T(1,128)} %bitcast.8, s32[1,512]{1,0:T(1,128)} %bitcast.9, bf16[512,8,128]{2,1,0:T(8,128)(2,1)} %proj.1, f32[64,32]{1,0:T(8,128)} %bitcast.7, ...), custom_call_target="tpu_custom_call" | custom-call | tf_op jit(solution)/shard_map/exchange_and_apply/pallas_call | solution.py:453
  44.0 3.2 %finish.1 = bf16[2,6,192,192]{3,2,1,0:T(8,128)(2,1)} custom-call(bf16[96,256]{1,0:T(8,128)(2,1)} %constant.13.clone.cyt, bf16[32,8,896]{2,1,0:T(8,128)(2,1)} %exchange_and_apply.1.recv, bf16[2,6,192,192]{3,2,1,0:T(8,128)(2,1)} %waves.3), custom_call_target="tpu_custom_call" | custom-call | tf_op jit(solution)/shard_map/finish/pallas_call | solution.py:515

commit v6 on v4

--- a/solution.py
+++ b/solution.py
@@ -99,11 +99,8 @@
 
     barrier = pltpu.get_barrier_semaphore()
 
-    def greet(d, carry):
+    for d in range(1, G):
         pl.semaphore_signal(barrier, inc=1, device_id={"grid": peer(d)}, device_id_type=MESH)
-        return carry
-
-    lax.fori_loop(1, G, greet, 0)
 
     @pl.when(active)
     def _():
@@ -127,26 +124,42 @@
 
     pl.semaphore_wait(barrier, G - 1)
 
+    my_row, place = g // A, lax.rem(g, A)
+    partner = lax.rem(g + A, G)
+
     def half(ref, i, plan, h):
         return ref.at[i, :, pl.ds(plan[h][0] * 128, plan[h][1] * 128)]
 
-    def first_copy(d, h):
-        to = peer(d)
+    def remote(src, dst, send, recv, to):
         return pltpu.make_async_remote_copy(
-            src_ref=half(send1, to, FIRST, h), dst_ref=half(recv1, ai, FIRST, h),
-            send_sem=s1.at[h, d], recv_sem=r1.at[h, ai],
+            src_ref=src, dst_ref=dst, send_sem=send, recv_sem=recv,
             device_id={"grid": to}, device_id_type=MESH,
         )
 
+    def whole(ref, count, plan, h, send, recv):
+        chunks = half(ref, pl.ds(0, count), plan, h)
+        return remote(chunks, chunks, send.at[h], recv.at[h], partner)
+
+    def first_copy(row, n, h):
+        to = row * A + lax.rem(place + n, A)
+        remote(
+            half(send1, to, FIRST, h), half(recv1, ai, FIRST, h), s1.at[h], r1.at[h], to
+        ).start()
+
     @pl.when(active)
     def _():
         for h in range(2):
 
-            def go(d, carry):
-                first_copy(d, h).start()
+            def across(n, carry):
+                first_copy(1 - my_row, n, h)
                 return carry
 
-            lax.fori_loop(1, G, go, 0)
+            def along(n, carry):
+                first_copy(my_row, n, h)
+                return carry
+
+            lax.fori_loop(0, A, across, 0)
+            lax.fori_loop(1, A, along, 0)
         recv1[ai] = send1[g]
 
     for copy in loads:
@@ -190,20 +203,13 @@
         potc[3 * j + 2] = o[:, 64:]
 
     def wait_first(h):
-        def body(i, carry):
-            src = jnp.where(i < 8, i, i + 16)
-
-            @pl.when(src != g)
-            def _():
-                pltpu.make_async_remote_copy(
-                    src_ref=half(send1, 0, FIRST, h), dst_ref=half(recv1, i, FIRST, h),
-                    send_sem=s1.at[h, 0], recv_sem=r1.at[h, i],
-                    device_id={"grid": src}, device_id_type=MESH,
-                ).wait_recv()
-
-            return carry
-
-        lax.fori_loop(0, A, body, 0)
+        @pl.when(active)
+        def _():
+            whole(recv1, A - 1, FIRST, h, s1, r1).wait_recv()
+
+        @pl.when(jnp.logical_not(active))
+        def _():
+            whole(recv1, A, FIRST, h, s1, r1).wait_recv()
 
     def arrived(h):
         wire, count, _ = FIRST[h]
@@ -278,14 +284,6 @@
                 )
         return lines
 
-    def second_copy(i, h):
-        to = jnp.where(i < 8, i, i + 16)
-        return to, pltpu.make_async_remote_copy(
-            src_ref=half(send2, i, SECOND, h), dst_ref=half(out, g, SECOND, h),
-            send_sem=s2.at[h, i], recv_sem=r2.at[h, g],
-            device_id={"grid": to}, device_id_type=MESH,
-        )
-
     def send_back(lines, h):
         wire, count, _ = SECOND[h]
         rows = [line[:, : count * 128] for line in lines]
@@ -299,12 +297,14 @@
         send2[:, :, wire * 128 : (wire + count) * 128] = jnp.swapaxes(rows, 0, 1).astype(BF16)
 
         def go(n, carry):
-            i = lax.rem(n + g, A)
-            to, copy = second_copy(i, h)
+            i = lax.rem(n + place, A)
+            to = jnp.where(i < 8, i, i + A)
 
             @pl.when(to != g)
             def _():
-                copy.start()
+                remote(
+                    half(send2, i, SECOND, h), half(out, g, SECOND, h), s2.at[h], r2.at[h], to
+                ).start()
 
             return carry
 
@@ -329,49 +329,42 @@
     def _():
         own = pltpu.make_async_copy(send2.at[ai], out.at[g], self_sem)
         own.start()
+        for h in range(2):
+            whole(send1, G - 1, FIRST, h, s1, r1).wait_send()
+            whole(send2, A - 1, SECOND, h, s2, r2).wait_send()
         own.wait()
         for h in range(2):
-
-            def wait_sent(d, carry):
-                first_copy(d, h).wait_send()
-                return carry
-
-            lax.fori_loop(1, G, wait_sent, 0)
-
-            def wait_second(src, carry):
-                @pl.when(src != g)
-                def _():
-                    pltpu.make_async_remote_copy(
-                        src_ref=half(send2, 0, SECOND, h), dst_ref=half(out, src, SECOND, h),
-                        send_sem=s2.at[h, 0], recv_sem=r2.at[h, src],
-                        device_id={"grid": src}, device_id_type=MESH,
-                    ).wait_recv()
-
-                return carry
-
-            lax.fori_loop(0, G, wait_second, 0)
-
-    for h in range(2):
-
-        def wait_back(i, carry):
-            to, copy = second_copy(i, h)
-
-            @pl.when(to != g)
-            def _():
-                copy.wait_send()
-
-            return carry
-
-        lax.fori_loop(0, A, wait_back, 0)
-
-
-def last_kernel(cyt, recv, waves, out):
+            whole(out, G - 1, SECOND, h, s2, r2).wait_recv()
+
+    @pl.when(jnp.logical_not(active))
+    def _():
+        for h in range(2):
+            whole(send2, A, SECOND, h, s2, r2).wait_send()
+
+
+def last_kernel(cyt, recv, waves, out, cyv, got_ref, wlo, whi, zero, low, high, load_sem, store_sem):
     g = lax.axis_index("grid")
     active = jnp.logical_or(g < 8, g >= 24)
 
     @pl.when(active)
     def _():
-        got = recv[...].astype(F32)
+        loads = [
+            pltpu.make_async_copy(a, b, load_sem.at[n])
+            for n, (a, b) in enumerate(
+                (
+                    (recv, got_ref), (cyt, cyv),
+                    (waves.at[:, :, 0:48, :], wlo), (waves.at[:, :, 144:192, :], whi),
+                )
+            )
+        ]
+        for copy in loads:
+            copy.start()
+        zero[...] = jnp.zeros(zero.shape, BF16)
+        stores = [pltpu.make_async_copy(zero, out.at[:, :, 48:144, :], store_sem.at[0])]
+        stores[0].start()
+        for copy in loads:
+            copy.wait()
+        got = got_ref[...].astype(F32)
         sub = lax.broadcasted_iota(jnp.int32, (G, 8, 128), 1)
         planes = []
         for wire, count, _ in SECOND:
@@ -382,31 +375,43 @@
                 spare = jnp.where(sub == y, tile(got, wire + y % count)[:, row : row + 1, :], spare)
             planes.append(spare)
         planes = jnp.concatenate(planes, axis=2).reshape(256, 1152).astype(BF16)
-        fifth = dot(cyt[...], planes)
-        for k in range(T):
-            ksq = sphere_sq(g * T + k)
-            inside = ksq < RAD2
-            kinetic = ksq.astype(F32) / RAD2
-            for b in range(2):
+        fifth = dot(cyv[...], planes)
+        for b in range(2):
+            for k in range(T):
+                ksq = sphere_sq(g * T + k)
                 n = (b * T + k) * 96
-                w = kept(waves[b, k, 0:48, :], waves[b, k, 144:192, :])
-                total = jnp.where(inside, kinetic * w + fifth[:, n : n + 96], 0.0)
-                wide = jnp.concatenate([total[:, :48], jnp.zeros((96, 96), F32), total[:, 48:]], axis=1)
-                wide = wide.astype(BF16)
-                out[b, k, 0:48, :] = wide[:48]
-                out[b, k, 48:144, :] = jnp.zeros((96, N), BF16)
-                out[b, k, 144:192, :] = wide[48:]
+                total = ksq.astype(F32) / RAD2 * kept(wlo[b, k], whi[b, k]) + fifth[:, n : n + 96]
+                total = jnp.where(ksq < RAD2, total, 0.0)
+                total = jnp.concatenate([total[:, :48], jnp.zeros((96, 96), F32), total[:, 48:]], axis=1)
+                total = total.astype(BF16)
+                low[b, k] = total[:48]
+                high[b, k] = total[48:]
+            stores += [
+                pltpu.make_async_copy(low.at[b], out.at[b, :, 0:48, :], store_sem.at[1 + 2 * b]),
+                pltpu.make_async_copy(high.at[b], out.at[b, :, 144:192, :], store_sem.at[2 + 2 * b]),
+            ]
+            stores[-2].start()
+            stores[-1].start()
+        for copy in stores:
+            copy.wait()
 
     @pl.when(jnp.logical_not(active))
     def _():
-        out[...] = jnp.zeros(out.shape, BF16)
+        zero[...] = jnp.zeros(zero.shape, BF16)
+        stores = [
+            pltpu.make_async_copy(zero, out.at[:, :, n * 96 : (n + 1) * 96, :], store_sem.at[n])
+            for n in range(2)
+        ]
+        for copy in stores:
+            copy.start()
+        for copy in stores:
+            copy.wait()
 
 
 def shards(waves, potential, block_index, atom_of_slot, projectors, coupling):
     cy, cyt, cx, cxt, wz, wzt = (jnp.asarray(x) for x in tables())
     coup = jnp.transpose(coupling, (1, 2, 0)).reshape(64, 32)
     hbm = pl.BlockSpec(memory_space=pltpu.HBM)
-    vmem = pl.BlockSpec(memory_space=pltpu.VMEM)
     dma = pltpu.SemaphoreType.DMA
     recv = pl.pallas_call(
         main_kernel,
@@ -442,10 +447,10 @@
             pltpu.VMEM((2, 8, 128), F32),
             pltpu.VMEM((2, 4, 8, 128), F32),
             dma((12,)),
-            dma((2, G)),
-            dma((2, A)),
-            dma((2, A)),
-            dma((2, G)),
+            dma((2,)),
+            dma((2,)),
+            dma((2,)),
+            dma((2,)),
             dma,
             dma((2, 4)),
             dma((2, 4)),
@@ -463,8 +468,19 @@
         last_kernel,
         name="finish",
         out_shape=jax.ShapeDtypeStruct(waves.shape, BF16),
-        in_specs=[vmem] * 3,
-        out_specs=vmem,
+        in_specs=[hbm] * 3,
+        out_specs=hbm,
+        scratch_shapes=[
+            pltpu.VMEM((96, 256), BF16),
+            pltpu.VMEM((G, 8, 896), BF16),
+            pltpu.VMEM((2, T, 48, N), BF16),
+            pltpu.VMEM((2, T, 48, N), BF16),
+            pltpu.VMEM((2, T, 96, N), BF16),
+            pltpu.VMEM((2, T, 48, N), BF16),
+            pltpu.VMEM((2, T, 48, N), BF16),
+            dma((4,)),
+            dma((5,)),
+        ],
         compiler_params=pltpu.CompilerParams(vmem_limit_bytes=60 << 20),
     )(cyt, recv, waves)
 

time: 45.8 us -> 43.6 us (0.952)
  Pallas kernels: 45.7 us -> 43.4 us
    pallas_call x1, Pallas kernels: 42.5 us -> 40.5 us  [shards(): pl.pallas_call(main_kernel, name='exchange_and_apply', out_shape=jax.Shap...]
where the time goes in v6:
time: 43.6 us; the launch traced here: 43.4 us
  Pallas kernels  43.4 us (100%)
    pallas_call x1, Pallas kernels, shards(): pl.pallas_call(main_kernel, name='exchange_and_apply', out_shape=jax.Shap...  40.5 us
    pallas_call x1, Pallas kernels, shards(): pl.pallas_call(last_kernel, name='finish', out_shape=jax.ShapeDtypeStruct...  2.88 us

profile of v6, /device:TPU:1, one launch (start us, length us, event | category | flops | bytes accessed | tf_op | source)
XLA Modules:
  0.0 43.4 jit_solution(3613352604543298182)
XLA Ops:
  0.0 40.5 %exchange_and_apply.1.recv = bf16[32,8,896]{2,1,0:T(8,128)(2,1)} custom-call(bf16[2,6,192,192]{3,2,1,0:T(8,128)(2,1)} %waves.3, bf16[6,192,192]{2,1,0:T(8,128)(2,1)} %bitcast.6, s32[1,512]{1,0:T(1,128)} %bitcast.8, s32[1,512]{1,0:T(1,128)} %bitcast.9, bf16[512,8,128]{2,1,0:T(8,128)(2,1)} %proj.1, f32[64,32]{1,0:T(8,128)} %bitcast.7, ...), custom_call_target="tpu_custom_call" | custom-call | tf_op jit(solution)/shard_map/exchange_and_apply/pallas_call | solution.py:416
  40.5 2.9 %finish.1 = bf16[2,6,192,192]{3,2,1,0:T(8,128)(2,1)} custom-call(bf16[96,256]{1,0:T(8,128)(2,1)} %constant.13.clone.cyt, bf16[32,8,896]{2,1,0:T(8,128)(2,1)} %exchange_and_apply.1.recv, bf16[2,6,192,192]{3,2,1,0:T(8,128)(2,1)} %waves.3), custom_call_target="tpu_custom_call" | custom-call | tf_op jit(solution)/shard_map/finish/pallas_call | solution.py:467

commit v7 on v6

--- a/solution.py
+++ b/solution.py
@@ -102,25 +102,31 @@
     for d in range(1, G):
         pl.semaphore_signal(barrier, inc=1, device_id={"grid": peer(d)}, device_id_type=MESH)
 
+    def transform(h):
+        parts = []
+        wire, count, begin = FIRST[h]
+        first, last = begin * 128 // 96, (begin + count + 1) * 128
+        for n in range(first, -(-last // 96)):
+            b, k = n // T, n % T
+            inside = sphere_sq(g * T + k) < RAD2
+            parts.append(jnp.where(inside, kept(wlo[b, k], whi[b, k]), 0.0))
+        rhs = jnp.concatenate(parts, axis=1)
+        skip = begin * 128 - first * 96
+        rhs = rhs[:, skip : skip + (count + 1) * 128].astype(BF16)
+        sub = lax.broadcasted_iota(jnp.int32, (G, 8, 128), 1)
+        spare = dot(cyv[...], tile(rhs, count)).reshape(G, 8, 128)
+        for t in range(count):
+            plane = dot(cyv[...], tile(rhs, t)).reshape(G, 8, 128)
+            for row, y in ((6, t), (7, t + count)):
+                if y < T:
+                    plane = jnp.where(sub == row, spare[:, y : y + 1, :], plane)
+            send1[:, :, (wire + t) * 128 : (wire + t + 1) * 128] = plane.astype(BF16)
+
     @pl.when(active)
     def _():
         for copy in wave_loads:
             copy.wait()
-        parts = []
-        for b in range(2):
-            for k in range(T):
-                inside = sphere_sq(g * T + k) < RAD2
-                parts.append(jnp.where(inside, kept(wlo[b, k], whi[b, k]), 0.0))
-        rhs = jnp.concatenate(parts, axis=1).astype(BF16)
-        sub = lax.broadcasted_iota(jnp.int32, (G, 8, 128), 1)
-        for wire, count, begin in FIRST:
-            spare = dot(cyv[...], tile(rhs, begin + count)).reshape(G, 8, 128)
-            for t in range(count):
-                plane = dot(cyv[...], tile(rhs, begin + t)).reshape(G, 8, 128)
-                for row, y in ((6, t), (7, t + count)):
-                    if y < T:
-                        plane = jnp.where(sub == row, spare[:, y : y + 1, :], plane)
-                send1[:, :, (wire + t) * 128 : (wire + t + 1) * 128] = plane.astype(BF16)
+        transform(0)
 
     pl.semaphore_wait(barrier, G - 1)
 
@@ -149,6 +155,8 @@
     @pl.when(active)
     def _():
         for h in range(2):
+            if h == 1:
+                transform(1)
 
             def across(n, carry):
                 first_copy(1 - my_row, n, h)
@@ -182,13 +190,13 @@
     def column(row):
         return jnp.transpose(jnp.broadcast_to(row.astype(F32), (128, 512))).astype(jnp.int32)
 
-    idx_col = column(idx_row)
-    idx_col = jnp.concatenate([idx_col, idx_col[:, :64]], axis=1)
-    lane192 = lax.broadcasted_iota(jnp.int32, (512, N), 1) * 9
+    idx_col = column(idx_row)[:, :1]
+    lane = lax.broadcasted_iota(jnp.int32, (1, 9 * N), 1)
+    ninth = lax.shift_right_logical(lane * 43691, 23)
+    oh1[...] = jnp.where((lane - ninth * N) * 9 + ninth == idx_col, 1.0, 0.0).astype(BF16)
     row192 = lax.broadcasted_iota(jnp.int32, (N, 512), 0) * 9
     for c in range(9):
-        oh1[c] = jnp.where(lane192 + c == idx_col, 1.0, 0.0).astype(BF16)
-        oh2[c] = jnp.where(row192 + c == idx_row, 1.0, 0.0).astype(BF16)
+        oh2[c * N : (c + 1) * N] = jnp.where(row192 + c == idx_row, 1.0, 0.0).astype(BF16)
     lane128 = lax.broadcasted_iota(jnp.int32, (512, 128), 1)
     oha[...] = jnp.where(column(atom_row) == lane128, 1.0, 0.0).astype(BF16)
     up_row = lax.broadcasted_iota(jnp.int32, (128, 1024), 0)
@@ -236,10 +244,9 @@
             part = dot(cxv[...], rhs).astype(BF16)
             real = dot(part, wzv[...]).astype(BF16)
             for t in range(3):
-                rs[b, 3 * j + t] = tile(real, t)
-        rows = dot(oh1[0], rs[b, 0])
-        for c in range(1, 9):
-            rows = rows + dot(oh1[c], rs[b, c])
+                c = 3 * j + t
+                rs[b, c * N : (c + 1) * N] = tile(real, t)
+        rows = dot(oh1[...], rs[b])
         prod = jnp.concatenate([(projt[p] * rows).astype(BF16) for p in range(8)], axis=1)
         inter = lax.dot_general(
             prod, exp_up[...], (((1,), (1,)), ((), ())), preferred_element_type=F32
@@ -269,11 +276,13 @@
         for p in range(1, 8):
             back = back + projt[p] * dot(chosen, tile(exp_up[...], p))
         back = back.astype(BF16)
+        spread = dot(oh2[...], back)
         lines = []
         for j in range(3):
             row = []
             for c in range(3 * j, 3 * j + 3):
-                row.append((potc[c] * rs[b, c].astype(F32) + dot(oh2[c], back)).astype(BF16))
+                cut = slice(c * N, (c + 1) * N)
+                row.append((potc[c] * rs[b, cut].astype(F32) + spread[cut]).astype(BF16))
             part = dot(jnp.concatenate(row, axis=1), wztv[...]).astype(BF16)
             part = dot(cxtv[...], part)
             for par in range(2):
@@ -434,13 +443,13 @@
             pltpu.VMEM((64, 32), F32),
             pltpu.VMEM((8, 512, 128), F32),
             pltpu.VMEM((9, N, 128), F32),
-            pltpu.VMEM((9, 512, N), BF16),
-            pltpu.VMEM((9, N, 512), BF16),
+            pltpu.VMEM((512, 9 * N), BF16),
+            pltpu.VMEM((9 * N, 512), BF16),
             pltpu.VMEM((512, 128), BF16),
             pltpu.VMEM((128, 1024), BF16),
             pltpu.VMEM((G, 8, 896), BF16),
             pltpu.VMEM((A, 8, 896), BF16),
-            pltpu.VMEM((2, 9, N, 128), BF16),
+            pltpu.VMEM((2, 9 * N, 128), BF16),
             pltpu.VMEM((A, 8, 896), BF16),
             pltpu.VMEM((64, 128), F32),
             pltpu.VMEM((2, 64, 128), F32),

time: 43.6 us -> 43 us (0.986)
  Pallas kernels: 43.4 us -> 42.8 us
    pallas_call x1, Pallas kernels: 40.5 us -> 39.9 us  [shards(): pl.pallas_call(main_kernel, name='exchange_and_apply', out_shape=jax.Shap...]
where the time goes in v7:
time: 43 us; the launch traced here: 42.8 us
  Pallas kernels  42.8 us (100%)
    pallas_call x1, Pallas kernels, shards(): pl.pallas_call(main_kernel, name='exchange_and_apply', out_shape=jax.Shap...  39.9 us
    pallas_call x1, Pallas kernels, shards(): pl.pallas_call(last_kernel, name='finish', out_shape=jax.ShapeDtypeStruct...  2.88 us

profile of v7, /device:TPU:1, one launch (start us, length us, event | category | flops | bytes accessed | tf_op | source)
XLA Modules:
  0.0 42.8 jit_solution(11936731261661878412)
XLA Ops:
  0.0 39.9 %exchange_and_apply.1.recv = bf16[32,8,896]{2,1,0:T(8,128)(2,1)} custom-call(bf16[2,6,192,192]{3,2,1,0:T(8,128)(2,1)} %waves.3, bf16[6,192,192]{2,1,0:T(8,128)(2,1)} %bitcast.6, s32[1,512]{1,0:T(1,128)} %bitcast.8, s32[1,512]{1,0:T(1,128)} %bitcast.9, bf16[512,8,128]{2,1,0:T(8,128)(2,1)} %proj.1, f32[64,32]{1,0:T(8,128)} %bitcast.7, ...), custom_call_target="tpu_custom_call" | custom-call | tf_op jit(solution)/shard_map/exchange_and_apply/pallas_call | solution.py:425
  39.9 2.9 %finish.1 = bf16[2,6,192,192]{3,2,1,0:T(8,128)(2,1)} custom-call(bf16[96,256]{1,0:T(8,128)(2,1)} %constant.13.clone.cyt, bf16[32,8,896]{2,1,0:T(8,128)(2,1)} %exchange_and_apply.1.recv, bf16[2,6,192,192]{3,2,1,0:T(8,128)(2,1)} %waves.3), custom_call_target="tpu_custom_call" | custom-call | tf_op jit(solution)/shard_map/finish/pallas_call | solution.py:476

commit v8 on v7

--- a/solution.py
+++ b/solution.py
@@ -94,13 +94,12 @@
         for copy in wave_loads:
             copy.start()
 
+    barrier = pltpu.get_barrier_semaphore()
+    for d in range(1, G):
+        pl.semaphore_signal(barrier, inc=1, device_id={"grid": peer(d)}, device_id_type=MESH)
+
     for copy in loads:
         copy.start()
-
-    barrier = pltpu.get_barrier_semaphore()
-
-    for d in range(1, G):
-        pl.semaphore_signal(barrier, inc=1, device_id={"grid": peer(d)}, device_id_type=MESH)
 
     def transform(h):
         parts = []
@@ -306,7 +305,7 @@
         send2[:, :, wire * 128 : (wire + count) * 128] = jnp.swapaxes(rows, 0, 1).astype(BF16)
 
         def go(n, carry):
-            i = lax.rem(n + place, A)
+            i = jnp.where(n < 8, 1 - my_row, my_row) * 8 + lax.rem(n + place, 8)
             to = jnp.where(i < 8, i, i + A)
 
             @pl.when(to != g)
@@ -371,7 +370,7 @@
         zero[...] = jnp.zeros(zero.shape, BF16)
         stores = [pltpu.make_async_copy(zero, out.at[:, :, 48:144, :], store_sem.at[0])]
         stores[0].start()
-        for copy in loads:
+        for copy in loads[:2]:
             copy.wait()
         got = got_ref[...].astype(F32)
         sub = lax.broadcasted_iota(jnp.int32, (G, 8, 128), 1)
@@ -385,6 +384,8 @@
             planes.append(spare)
         planes = jnp.concatenate(planes, axis=2).reshape(256, 1152).astype(BF16)
         fifth = dot(cyv[...], planes)
+        for copy in loads[2:]:
+            copy.wait()
         for b in range(2):
             for k in range(T):
                 ksq = sphere_sq(g * T + k)

time: 43 us -> 43.5 us (1.012)
  Pallas kernels: 42.8 us -> 43.4 us
    pallas_call x1, Pallas kernels: 2.88 us -> 3.35 us  [shards(): pl.pallas_call(last_kernel, name='finish', out_shape=jax.ShapeDtypeStruct...]
where the time goes in v8:
time: 43.5 us; the launch traced here: 43.4 us
  Pallas kernels  43.4 us (100%)
    pallas_call x1, Pallas kernels, shards(): pl.pallas_call(main_kernel, name='exchange_and_apply', out_shape=jax.Shap...  40 us
    pallas_call x1, Pallas kernels, shards(): pl.pallas_call(last_kernel, name='finish', out_shape=jax.ShapeDtypeStruct...  3.35 us

profile of v8, /device:TPU:1, one launch (start us, length us, event | category | flops | bytes accessed | tf_op | source)
XLA Modules:
  0.0 43.4 jit_solution(14777262700732012662)
XLA Ops:
  0.0 40.0 %exchange_and_apply.1.recv = bf16[32,8,896]{2,1,0:T(8,128)(2,1)} custom-call(bf16[2,6,192,192]{3,2,1,0:T(8,128)(2,1)} %waves.3, bf16[6,192,192]{2,1,0:T(8,128)(2,1)} %bitcast.6, s32[1,512]{1,0:T(1,128)} %bitcast.8, s32[1,512]{1,0:T(1,128)} %bitcast.9, bf16[512,8,128]{2,1,0:T(8,128)(2,1)} %proj.1, f32[64,32]{1,0:T(8,128)} %bitcast.7, ...), custom_call_target="tpu_custom_call" | custom-call | tf_op jit(solution)/shard_map/exchange_and_apply/pallas_call | solution.py:426
  40.0 3.4 %finish.1 = bf16[2,6,192,192]{3,2,1,0:T(8,128)(2,1)} custom-call(bf16[96,256]{1,0:T(8,128)(2,1)} %constant.13.clone.cyt, bf16[32,8,896]{2,1,0:T(8,128)(2,1)} %exchange_and_apply.1.recv, bf16[2,6,192,192]{3,2,1,0:T(8,128)(2,1)} %waves.3), custom_call_target="tpu_custom_call" | custom-call | tf_op jit(solution)/shard_map/finish/pallas_call | solution.py:477

commit v9 on v8

--- a/solution.py
+++ b/solution.py
@@ -305,7 +305,7 @@
         send2[:, :, wire * 128 : (wire + count) * 128] = jnp.swapaxes(rows, 0, 1).astype(BF16)
 
         def go(n, carry):
-            i = jnp.where(n < 8, 1 - my_row, my_row) * 8 + lax.rem(n + place, 8)
+            i = lax.rem(n + place, A)
             to = jnp.where(i < 8, i, i + A)
 
             @pl.when(to != g)

time: 43.5 us -> 43.4 us (level)
  no operation moved by 1% of the time
where the time goes in v9:
time: 43.4 us; the launch traced here: 43.3 us
  Pallas kernels  43.2 us (100%)
    pallas_call x1, Pallas kernels, shards(): pl.pallas_call(main_kernel, name='exchange_and_apply', out_shape=jax.Shap...  39.9 us
    pallas_call x1, Pallas kernels, shards(): pl.pallas_call(last_kernel, name='finish', out_shape=jax.ShapeDtypeStruct...  3.35 us

profile of v9, /device:TPU:1, one launch (start us, length us, event | category | flops | bytes accessed | tf_op | source)
XLA Modules:
  0.0 43.3 jit_solution(16399871937866053847)
XLA Ops:
  0.0 39.9 %exchange_and_apply.1.recv = bf16[32,8,896]{2,1,0:T(8,128)(2,1)} custom-call(bf16[2,6,192,192]{3,2,1,0:T(8,128)(2,1)} %waves.3, bf16[6,192,192]{2,1,0:T(8,128)(2,1)} %bitcast.6, s32[1,512]{1,0:T(1,128)} %bitcast.8, s32[1,512]{1,0:T(1,128)} %bitcast.9, bf16[512,8,128]{2,1,0:T(8,128)(2,1)} %proj.1, f32[64,32]{1,0:T(8,128)} %bitcast.7, ...), custom_call_target="tpu_custom_call" | custom-call | tf_op jit(solution)/shard_map/exchange_and_apply/pallas_call | solution.py:426
  39.9 3.4 %finish.1 = bf16[2,6,192,192]{3,2,1,0:T(8,128)(2,1)} custom-call(bf16[96,256]{1,0:T(8,128)(2,1)} %constant.13.clone.cyt, bf16[32,8,896]{2,1,0:T(8,128)(2,1)} %exchange_and_apply.1.recv, bf16[2,6,192,192]{3,2,1,0:T(8,128)(2,1)} %waves.3), custom_call_target="tpu_custom_call" | custom-call | tf_op jit(solution)/shard_map/finish/pallas_call | solution.py:477

commit v10 on v7

--- a/solution.py
+++ b/solution.py
@@ -306,7 +306,7 @@
         send2[:, :, wire * 128 : (wire + count) * 128] = jnp.swapaxes(rows, 0, 1).astype(BF16)
 
         def go(n, carry):
-            i = lax.rem(n + place, A)
+            i = jnp.where(n < 8, 1 - my_row, my_row) * 8 + lax.rem(n + place, 8)
             to = jnp.where(i < 8, i, i + A)
 
             @pl.when(to != g)

time: 43 us -> 43.1 us (level)
  no operation moved by 1% of the time
where the time goes in v10:
time: 43.1 us; the launch traced here: 42.9 us
  Pallas kernels  42.9 us (100%)
    pallas_call x1, Pallas kernels, shards(): pl.pallas_call(main_kernel, name='exchange_and_apply', out_shape=jax.Shap...  40.1 us
    pallas_call x1, Pallas kernels, shards(): pl.pallas_call(last_kernel, name='finish', out_shape=jax.ShapeDtypeStruct...  2.88 us

profile of v10, /device:TPU:1, one launch (start us, length us, event | category | flops | bytes accessed | tf_op | source)
XLA Modules:
  0.0 42.9 jit_solution(11921070105238035774)
XLA Ops:
  0.0 40.1 %exchange_and_apply.1.recv = bf16[32,8,896]{2,1,0:T(8,128)(2,1)} custom-call(bf16[2,6,192,192]{3,2,1,0:T(8,128)(2,1)} %waves.3, bf16[6,192,192]{2,1,0:T(8,128)(2,1)} %bitcast.6, s32[1,512]{1,0:T(1,128)} %bitcast.8, s32[1,512]{1,0:T(1,128)} %bitcast.9, bf16[512,8,128]{2,1,0:T(8,128)(2,1)} %proj.1, f32[64,32]{1,0:T(8,128)} %bitcast.7, ...), custom_call_target="tpu_custom_call" | custom-call | tf_op jit(solution)/shard_map/exchange_and_apply/pallas_call | solution.py:425
  40.1 2.9 %finish.1 = bf16[2,6,192,192]{3,2,1,0:T(8,128)(2,1)} custom-call(bf16[96,256]{1,0:T(8,128)(2,1)} %constant.13.clone.cyt, bf16[32,8,896]{2,1,0:T(8,128)(2,1)} %exchange_and_apply.1.recv, bf16[2,6,192,192]{3,2,1,0:T(8,128)(2,1)} %waves.3), custom_call_target="tpu_custom_call" | custom-call | tf_op jit(solution)/shard_map/finish/pallas_call | solution.py:476

commit v11 on v7

--- a/solution.py
+++ b/solution.py
@@ -130,7 +130,7 @@
 
     pl.semaphore_wait(barrier, G - 1)
 
-    my_row, place = g // A, lax.rem(g, A)
+    place = lax.rem(g, A)
     partner = lax.rem(g + A, G)
 
     def half(ref, i, plan, h):
@@ -146,8 +146,8 @@
         chunks = half(ref, pl.ds(0, count), plan, h)
         return remote(chunks, chunks, send.at[h], recv.at[h], partner)
 
-    def first_copy(row, n, h):
-        to = row * A + lax.rem(place + n, A)
+    def first_copy(d, h):
+        to = peer(d)
         remote(
             half(send1, to, FIRST, h), half(recv1, ai, FIRST, h), s1.at[h], r1.at[h], to
         ).start()
@@ -158,16 +158,11 @@
             if h == 1:
                 transform(1)
 
-            def across(n, carry):
-                first_copy(1 - my_row, n, h)
+            def go(d, carry):
+                first_copy(d, h)
                 return carry
 
-            def along(n, carry):
-                first_copy(my_row, n, h)
-                return carry
-
-            lax.fori_loop(0, A, across, 0)
-            lax.fori_loop(1, A, along, 0)
+            lax.fori_loop(1, G, go, 0)
         recv1[ai] = send1[g]
 
     for copy in loads:

time: 43 us -> 42.8 us (level)
  no operation moved by 1% of the time
where the time goes in v11:
time: 42.8 us; the launch traced here: 42.7 us
  Pallas kernels  42.6 us (100%)
    pallas_call x1, Pallas kernels, shards(): pl.pallas_call(main_kernel, name='exchange_and_apply', out_shape=jax.Shap...  39.8 us
    pallas_call x1, Pallas kernels, shards(): pl.pallas_call(last_kernel, name='finish', out_shape=jax.ShapeDtypeStruct...  2.88 us

profile of v11, /device:TPU:1, one launch (start us, length us, event | category | flops | bytes accessed | tf_op | source)
XLA Modules:
  0.0 42.7 jit_solution(17790822598718331496)
XLA Ops:
  0.0 39.8 %exchange_and_apply.1.recv = bf16[32,8,896]{2,1,0:T(8,128)(2,1)} custom-call(bf16[2,6,192,192]{3,2,1,0:T(8,128)(2,1)} %waves.3, bf16[6,192,192]{2,1,0:T(8,128)(2,1)} %bitcast.6, s32[1,512]{1,0:T(1,128)} %bitcast.8, s32[1,512]{1,0:T(1,128)} %bitcast.9, bf16[512,8,128]{2,1,0:T(8,128)(2,1)} %proj.1, f32[64,32]{1,0:T(8,128)} %bitcast.7, ...), custom_call_target="tpu_custom_call" | custom-call | tf_op jit(solution)/shard_map/exchange_and_apply/pallas_call | solution.py:420
  39.8 2.9 %finish.1 = bf16[2,6,192,192]{3,2,1,0:T(8,128)(2,1)} custom-call(bf16[96,256]{1,0:T(8,128)(2,1)} %constant.13.clone.cyt, bf16[32,8,896]{2,1,0:T(8,128)(2,1)} %exchange_and_apply.1.recv, bf16[2,6,192,192]{3,2,1,0:T(8,128)(2,1)} %waves.3), custom_call_target="tpu_custom_call" | custom-call | tf_op jit(solution)/shard_map/finish/pallas_call | solution.py:471
